TPU v7x, 128 devices: a whole 4x4x4 slice. The times are simulated.
128 devices in a mesh: dp: 8 (over x_lo, z), space: 16 (over y, x_hi, core).
Axes of the slice: x: 4 (x_hi: 2, x_lo: 2; x = x_hi * 2 + x_lo), y: 4, z: 4, core: 2. Of those that a mesh axis runs over, the one named last changes fastest.
Arguments:
- features: bfloat16 [8, 96, 16, 112, 448], P('dp', None, None, 'space'), may hold values from -6 to 6
- conv_weight: bfloat16 [3, 3, 3, 3, 96], replicated, may hold values from -0.125 to 0.125
- out_grad: bfloat16 [8, 16, 256, 384], P('dp', 'space'), may hold values from -6 to 6
- pos_embed: bfloat16 [256, 384], replicated, may hold values from -3 to 3
- patch_weight: bfloat16 [588, 384], replicated, may hold values from -0.25 to 0.25
- norm1: float32 [384], replicated, may hold values from 0.1 to 1.9
- qkv_weight: bfloat16 [384, 1152], replicated, may hold values from -0.3125 to 0.3125
- proj_weight: bfloat16 [384, 384], replicated, may hold values from -0.3125 to 0.3125
- norm2: float32 [384], replicated, may hold values from 0.1 to 1.9
- fc1_weight: bfloat16 [384, 1536], replicated, may hold values from -0.3125 to 0.3125
- fc2_weight: bfloat16 [1536, 384], replicated, may hold values from -0.15625 to 0.15625
Outputs:
- block_out: bfloat16 [8, 16, 256, 384], P('dp', 'space')
- feature_grad: bfloat16 [8, 96, 16, 112, 448], P('dp', None, None, 'space')
- conv_grad: float32 [3, 3, 3, 3, 96], replicated
- qkv_grad: float32 [384, 1152], P('space')
- proj_grad: float32 [384, 384], P('space')
- fc1_grad: float32 [384, 1536], P('space')
- fc2_grad: float32 [1536, 384], P('space')
All inputs are finite; a program needn't handle non-finite values.
Results may differ from a plain program's by a relative error of at most 0.025.
Values may be sent and summed in bfloat16 or wider, within the bound.
A program may use at most 192 MiB of HBM per device.

v0:
```python
import jax
import jax.numpy as jnp
from jax import lax
from jax.sharding import PartitionSpec as P

HEADS = 6


def shifted_2(block, axis, distance):
    devices = range(lax.axis_size(axis))
    route = [(i - distance, i) for i in devices if i - distance in devices]
    return lax.ppermute(block, axis, route)


def padded_2(cells, sides, width):
    for axis, dim in sides:
        count = lax.axis_size(axis)
        ends = count - 1
        head = lax.slice_in_dim(cells, 0, width, axis=dim)
        tail = lax.slice_in_dim(cells, cells.shape[dim] - width, cells.shape[dim], axis=dim)
        cells = jnp.concatenate(
            [
                lax.ppermute(tail, axis, [(i, (i + 1) % count) for i in range(ends)]),
                cells,
                lax.ppermute(head, axis, [((i + 1) % count, i) for i in range(ends)]),
            ],
            axis=dim,
        )
    return cells


def in_blocks(x, dim, length):
    shape = x.shape
    blocks = x.reshape(*shape[:dim], length, shape[dim] // length, *shape[dim + 1 :])
    return jnp.moveaxis(blocks, dim, 0)


def one_scatter(arrays, axis, dims):
    length = lax.axis_size(axis)
    blocks = [in_blocks(a, dim, length) for a, dim in zip(arrays, dims)]
    lines = jnp.concatenate([b.reshape(length, -1) for b in blocks], axis=1)
    extent = max(16, -(-lines.shape[1] // 1024) * 8)
    lines = jnp.pad(lines, ((0, 0), (0, extent * 128 - lines.shape[1]))).reshape(-1, 128)
    ravelled, at, finished = (lax.psum_scatter(lines, axis, tiled=True).reshape(-1), 0, [])
    for b in blocks:
        part = b[0]
        finished.append(ravelled[at : at + part.size].reshape(part.shape))
        at += part.size
    return tuple(finished)


def from_everyone(x, axis):
    copies = jnp.broadcast_to(x, (lax.axis_size(axis), *x.shape))
    return lax.all_to_all(copies, axis, split_axis=0, concat_axis=0, tiled=True)


def over_copies(x, axis):
    return from_everyone(x, axis).sum(axis=0)


def over_copies_2(x, axis):
    everything = from_everyone(x, axis)
    return jnp.sum(everything.astype(jnp.float32), axis=0)


def layer_norm(values, gain_vec):
    average = jnp.mean(values, axis=-1, keepdims=True)
    centered = values - average
    variance = jnp.mean(centered * centered, axis=-1, keepdims=True)
    return centered * lax.rsqrt(variance + 1e-06) * gain_vec


def discriminator(
    pixels, pos_embed, patch_weight, norm1, qkv_weight, proj_weight, norm2, fc1_weight, fc2_weight
):
    channels, height, width = pixels.shape
    patch_rows = height // 14
    patch_cols = width // 14
    count = patch_rows * patch_cols
    patches = (
        pixels.reshape(channels, patch_rows, 14, patch_cols, 14)
        .transpose(1, 3, 0, 2, 4)
        .reshape(count, channels * 196)
    )
    embedded = jnp.dot(
        patches, patch_weight, preferred_element_type=jnp.float32
    ) + pos_embed.astype(jnp.float32)
    model_width = embedded.shape[1]
    normed = layer_norm(embedded, norm1).astype(jnp.bfloat16)
    packed = jnp.dot(normed, qkv_weight, preferred_element_type=jnp.float32).astype(jnp.bfloat16)
    packed = packed.reshape(count, 3, HEADS, model_width // HEADS)
    queries = packed[:, 0]
    keys_in = packed[:, 1]
    values_in = packed[:, 2]
    head_size = model_width // HEADS
    scores = jnp.einsum("qhd,khd->hqk", queries, keys_in, preferred_element_type=jnp.float32) * (
        1.0 / float(head_size) ** 0.5
    )
    probs = jax.nn.softmax(scores, axis=-1).astype(jnp.bfloat16)
    attended = jnp.einsum("hqk,khd->qhd", probs, values_in, preferred_element_type=jnp.float32)
    attended = attended.astype(jnp.bfloat16).reshape(count, model_width)
    residual = embedded + jnp.dot(attended, proj_weight, preferred_element_type=jnp.float32)
    normed_two = layer_norm(residual, norm2).astype(jnp.bfloat16)
    hidden = jax.nn.gelu(
        jnp.dot(normed_two, fc1_weight, preferred_element_type=jnp.float32), approximate=False
    ).astype(jnp.bfloat16)
    return residual + jnp.dot(hidden, fc2_weight, preferred_element_type=jnp.float32)


def frame_steps(frames, cotangents, params):
    pos_embed, patch_weight, norm1, qkv_weight, proj_weight, norm2, fc1_weight, fc2_weight = params

    def one_frame(pixels, cotangent):

        def forward(pix, qkv_w, proj_w, fc1_w, fc2_w):
            return discriminator(
                pix, pos_embed, patch_weight, norm1, qkv_w, proj_w, norm2, fc1_w, fc2_w
            )

        result, pullback = jax.vjp(forward, pixels, qkv_weight, proj_weight, fc1_weight, fc2_weight)
        cotans = pullback(cotangent.astype(jnp.float32))
        return (
            result.astype(jnp.bfloat16),
            cotans[0],
            tuple((item.astype(jnp.float32) for item in cotans[1:])),
        )

    block_out, pixel_grads, weight_grads = jax.vmap(one_frame, in_axes=(1, 0), out_axes=(0, 1, 0))(
        frames, cotangents
    )
    return (block_out, pixel_grads, tuple((jnp.sum(item, axis=0) for item in weight_grads)))


def project_taps(feature_tile, tap_matrix):
    return lax.dot_general(
        tap_matrix, feature_tile, (((1,), (0,)), ((), ())), preferred_element_type=jnp.float32
    )


def time_parts(tap_values):
    grouped = tap_values.reshape((3, 3, 9) + tap_values.shape[1:])
    frame_count = tap_values.shape[1]
    parts = []
    for row_tap in range(3):
        total = None
        for time_tap in range(3):
            piece = grouped[time_tap, row_tap]
            lag = 2 - time_tap
            if lag > 0:
                piece = jnp.pad(piece[:, : frame_count - lag], ((0, 0), (lag, 0), (0, 0), (0, 0)))
            total = piece if total is None else total + piece
        parts.append(total)
    return parts


def column_sum(planes):
    width = planes.shape[-1]
    padded = jnp.pad(planes, ((0, 0), (0, 0), (0, 0), (1, 1)))
    return (
        padded[0:3, :, :, 0:width]
        + padded[3:6, :, :, 1 : 1 + width]
        + padded[6:9, :, :, 2 : 2 + width]
    )


def gather_taps(padded_grad, frame_count, row_count, col_count):
    shifted = [padded_grad[:, :, :, 2 - col_tap : 2 - col_tap + col_count] for col_tap in range(3)]
    pieces = []
    for time_tap in range(3):
        for row_tap in range(3):
            for col_tap in range(3):
                pieces.append(
                    shifted[col_tap][
                        :,
                        2 - time_tap : 2 - time_tap + frame_count,
                        2 - row_tap : 2 - row_tap + row_count,
                    ]
                )
    return jnp.stack(pieces, axis=0).reshape(-1, frame_count * row_count * col_count)


def conv_backward(stacked, feature_tile, tap_matrix):
    channels = feature_tile.shape[0]
    flat = feature_tile.reshape(channels, -1)
    feature_grad = lax.dot_general(
        tap_matrix, stacked, (((0,), (0,)), ((), ())), preferred_element_type=jnp.float32
    )
    feature_grad = feature_grad.reshape(feature_tile.shape).astype(jnp.bfloat16)
    conv_part = lax.dot_general(
        stacked, flat, (((1,), (1,)), ((), ())), preferred_element_type=jnp.float32
    )
    return (feature_grad, conv_part)


def shards(
    features,
    conv_weight,
    out_grad,
    pos_embed,
    patch_weight,
    norm1,
    qkv_weight,
    proj_weight,
    norm2,
    fc1_weight,
    fc2_weight,
):
    params = (
        pos_embed,
        patch_weight,
        norm1,
        qkv_weight,
        proj_weight,
        norm2,
        fc1_weight,
        fc2_weight,
    )
    feature_tile = features[0]
    channels, frame_count, tile_rows, tile_cols = feature_tile.shape
    tap_matrix = conv_weight.reshape(-1, channels)
    parts = time_parts(project_taps(feature_tile, tap_matrix))
    planes = None
    for row_tap in range(3):
        piece = jnp.pad(parts[row_tap], ((0, 0), (0, 0), (2, 2), (0, 0)))[
            :, :, row_tap : row_tap + tile_rows + 2
        ]
        planes = piece if planes is None else planes + piece
    extended = column_sum(planes)
    from_above = shifted_2(
        extended[:, :, tile_rows + 1 : tile_rows + 2].astype(jnp.bfloat16), "space", 1
    ).astype(jnp.float32)
    from_below = shifted_2(extended[:, :, 0:1].astype(jnp.bfloat16), "space", -1).astype(
        jnp.float32
    )
    summed = extended[:, :, 1 : tile_rows + 1]
    summed = summed + jnp.pad(from_above, ((0, 0), (0, 0), (0, tile_rows - 1), (0, 0)))
    summed = summed + jnp.pad(from_below, ((0, 0), (0, 0), (tile_rows - 1, 0), (0, 0)))
    pixels = summed.astype(jnp.bfloat16)
    frames = lax.all_to_all(pixels, "space", split_axis=1, concat_axis=2, tiled=True)
    block_out, pixel_grads, weight_grads = frame_steps(frames, out_grad[0], params)
    grad_tile = lax.all_to_all(pixel_grads, "space", split_axis=2, concat_axis=1, tiled=True)
    rimmed = padded_2(grad_tile, (("space", 2),), 1)
    padded_grad = jnp.pad(rimmed, ((0, 0), (0, 2), (0, 0), (1, 1)))
    stacked = gather_taps(padded_grad, frame_count, tile_rows, tile_cols)
    feature_grad, conv_part = conv_backward(stacked, feature_tile, tap_matrix)
    local_shares = tuple(
        (
            part.astype(jnp.float32)
            for part in one_scatter(
                (
                    weight_grads[0].astype(jnp.bfloat16),
                    weight_grads[1].astype(jnp.bfloat16),
                    weight_grads[2].astype(jnp.bfloat16),
                    weight_grads[3].astype(jnp.bfloat16),
                ),
                "space",
                (0, 0, 0, 0),
            )
        )
    )
    conv_space = over_copies(conv_part, "space")
    merged = (
        over_copies_2(local_shares[0].astype(jnp.bfloat16), "dp").astype(jnp.float32),
        over_copies_2(local_shares[1].astype(jnp.bfloat16), "dp").astype(jnp.float32),
        over_copies_2(local_shares[2].astype(jnp.bfloat16), "dp").astype(jnp.float32),
        over_copies_2(local_shares[3].astype(jnp.bfloat16), "dp").astype(jnp.float32),
        over_copies_2(conv_space.astype(jnp.bfloat16), "dp").astype(jnp.float32),
    )
    shares = (merged[0], merged[1], merged[2], merged[3])
    conv_total = merged[4]
    return (
        block_out[None],
        feature_grad[None],
        conv_total.reshape(conv_weight.shape),
        shares[0],
        shares[1],
        shares[2],
        shares[3],
    )


def solution(mesh):
    placed = (
        P("dp", None, None, "space", None),
        P(),
        P("dp", "space", None, None),
        P(),
        P(),
        P(),
        P(),
        P(),
        P(),
        P(),
        P(),
    )
    return jax.shard_map(
        shards,
        mesh=mesh,
        in_specs=placed,
        out_specs=(
            P("dp", "space", None, None),
            P("dp", None, None, "space", None),
            P(),
            P("space", None),
            P("space", None),
            P("space", None),
            P("space", None),
        ),
        check_vma=False,
    )
```

profile of v0, /device:TPU:0, one launch (start us, length us, event | category | flops | bytes accessed | tf_op | source)
XLA Modules:
  0.0 425.5 jit_solution(1263518016065582368)
XLA Ops:
  8.0 37.1 %fusion.2 = f32[3,3,9,16,7,448]{5,2,4,3,1,0:T(8,128)} fusion(bf16[96,16,7,448,1,1]{3,1,2,0,5,4:T(8,128)(2,1)} %bitcast.288, bf16[3,3,9,96,1,1]{3,1,2,0,5,4:T(4,128)(2,1)S(1)} %bitcast.308), kind=kOutput, calls=%fused_computation.3 | convolution fusion | flops 780337152 | bytes 25906368 | tf_op jit(solution)/shard_map/dot_general | solution.py:135
  45.1 17.1 %fusion.96 = (f32[1,1,9,16,7,448]{5,2,4,3,1,0:T(8,128)}, f32[1,1,9,16,7,448]{5,2,4,3,1,0:T(8,128)}, f32[1,1,9,16,7,448]{5,2,4,3,1,0:T(8,128)S(1)}, f32[1,1,9,16,...) fusion(f32[3,3,9,16,7,448]{5,2,4,3,1,0:T(8,128)} %fusion.2), kind=kLoop, calls=%fused_computation.199 | loop fusion | bytes 32514048 | tf_op jit(solution)/shard_map/slice | solution.py:147
  62.2 3.4 copy.185
  65.6 2.5 copy.186
  68.2 2.5 copy.187
  70.7 2.5 copy.188
  73.2 2.4 copy_bitcast_fusion.7
  75.5 3.3 fusion.12
  78.8 20.2 %fusion.10 = (f32[9,16,7,448]{3,1,2,0:T(8,128)}, f32[9,16,7,448]{3,1,2,0:T(8,128)}) fusion(f32[1,1,9,16,7,448]{5,2,4,3,1,0:T(8,128)} %get-tuple-element.65, f32[9,15,7,448]{3,1,2,0:T(8,128)S(1)} %bitcast.291, f32[9,14,7,448]{3,1,2,0:T(8,128)} %bitcast.292, f32[1,1,9,16,7,448]{5,2,4,3,1,0:T(8,128)S(1)} %get-tuple-element.59, f32[9,15,7,448]{3,1,2,0:T(8,128)} %bitcast.293, ...), kind=kLoop, calls=%fused_computation.26 | loop fusion | flops 1806336 | bytes 13773312 | tf_op jit(solution)/shard_map/add | solution.py:151
  99.0 3.6 fusion.5
  103.1 1.3 collective-permute-start
  104.4 1.3 collective-permute-start.1
  105.7 5.2 %collective-permute-done.1 = bf16[3,16,1,448]{3,1,2,0:T(8,128)(2,1)S(1)} collective-permute-done((bf16[3,16,1,448]{3,1,2,0:T(8,128)(2,1)S(1)}, bf16[3,16,1,448]{3,1,2,0:T(8,128)(2,1)S(1)}, u32[]{:S(2)}, u32[]{:S(2)}) %collective-permute-start.1) | collective-permute-done | bytes 43040 | tf_op jit(solution)/shard_map/ppermute | solution.py:12
  111.9 10.0 %all-to-all-start = ((bf16[3,16,7,448]{3,2,0,1:T(8,128)(2,1)}), bf16[3,16,7,448]{3,2,0,1:T(8,128)(2,1)S(1)}, u32[]{:S(2)}, u32[]{:S(2)}) async-start(bf16[3,16,7,448]{3,2,0,1:T(8,128)(2,1)} %copy.122), calls=%async_computation | async-start | bytes 786432 | tf_op jit(solution)/shard_map/all_to_all | solution.py:239
  122.0 13.7 %copy.135 = bf16[1,96,16,7,448]{4,3,2,1,0:T(8,128)(2,1)} copy(bf16[1,96,16,7,448]{4,2,3,1,0:T(8,128)(2,1)} %param.11) | data formatting | bytes 19267584 | tf_op args[0]
  135.6 17.8 %reshape_squeeze.3 = bf16[96,50176]{1,0:T(8,128)(2,1)} reshape(bf16[1,96,16,7,448]{4,3,2,1,0:T(8,128)(2,1)} %copy.135) | data formatting | bytes 19267584 | tf_op jit(solution)/shard_map/reshape;squeeze | solution.py:184
  153.5 7.5 %transpose.61 = bf16[1,3,8,14,32,14]{5,4,3,2,1,0:T(8,128)(2,1)} reshape(bf16[3,16,7,448]{3,2,1,0:T(8,128)(2,1)S(1)} %copy.123) | data formatting | bytes 602112 | tf_op jit(solution)/shard_map/vmap(jvp())/reshape;vmap(jvp())/transpose | solution.py:81
  161.0 4.0 copy.124
  165.0 1.5 reshape.462
  166.6 1.6 fusion.100
  169.2 1.8 fusion.101
  171.0 1.6 divide_convert_fusion
  173.6 5.1 %multiply_convert_fusion = (bf16[256,1536]{1,0:T(8,128)(2,1)}, f32[256,1536]{1,0:T(8,128)S(1)}, f32[256,1536]{1,0:T(8,128)S(1)}) fusion(bf16[384,1536]{1,0:T(8,128)(2,1)S(1)} %copy-done, f32[256,384]{1,0:T(8,128)S(1)} %get-tuple-element.77, f32[384]{0:T(512)S(1)} %copy-done.26, f32[256]{0:T(256)S(1)} %fusion.85, f32[256]{0:T(256)S(1)} %broadcast_multiply_fusion), kind=kOutput, calls=%fused_computation.53 | convolution fusion | flops 327942144 | bytes 5508608 | tf_op jit(solution)/shard_map/vmap(jvp())/dot_general | solution.py:105
  179.7 1.7 fusion.6
  183.2 1.8 fusion.23
  185.1 1.1 fusion.39
  186.2 1.1 fusion.40
  187.4 1.5 fusion.8
  188.9 1.3 multiply_reduce_fusion
  190.2 1.4 copy.140
  191.6 2.5 convert_element_type.288
  194.1 1.5 copy.138
  195.6 2.6 convert_element_type.280
  199.5 3.5 copy.131
  202.9 5.6 %reshape.472 = bf16[3,1,112,448]{3,2,0,1:T(8,128)(2,1)S(1)} reshape(bf16[1,3,8,14,32,14]{5,4,3,2,1,0:T(8,128)(2,1)} %bitcast.290) | data formatting | bytes 602112 | tf_op jit(solution)/shard_map/vmap()/transpose;vmap(transpose(jvp()))/reshape | solution.py:128
  208.6 1.1 copy.132
  209.7 7.6 %all-to-all-start.1 = ((bf16[3,1,112,448]{3,0,1,2:T(4,128)(2,1)}), bf16[3,1,112,448]{3,0,1,2:T(4,128)(2,1)}, u32[]{:S(2)}, u32[]{:S(2)}) async-start(bf16[3,1,112,448]{3,0,1,2:T(4,128)(2,1)} %copy.132), calls=%async_computation.1 | async-start | bytes 917504 | tf_op jit(solution)/shard_map/all_to_all | solution.py:241
  218.8 1.6 fusion.7
  220.4 1.7 convert_element_type.293
  222.2 6.8 %all-to-all-done.1 = bf16[3,1,112,448]{3,0,1,2:T(4,128)(2,1)} async-done(((bf16[3,1,112,448]{3,0,1,2:T(4,128)(2,1)}), bf16[3,1,112,448]{3,0,1,2:T(4,128)(2,1)}, u32[]{:S(2)}, u32[]{:S(2)}) %all-to-all-start.1) | async-done | bytes 301088 | tf_op jit(solution)/shard_map/all_to_all | solution.py:241
  228.9 1.2 copy.152
  230.9 1.3 collective-permute-start.2
  232.2 1.3 collective-permute-start.3
  233.5 1.9 pad_maximum_fusion
  235.4 4.3 %reshape.476 = bf16[13824,128]{1,0:T(8,128)(2,1)} reshape(bf16[16,110592]{1,0:T(8,128)(2,1)} %pad_maximum_fusion) | data formatting | bytes 7077888 | tf_op jit(solution)/shard_map/reshape | solution.py:43
  239.8 1.9 fusion.43
  259.3 1.9 fusion.58
  263.1 1.9 copy_dynamic-update-slice_fusion
  268.5 16.4 %reshape.473 = bf16[81,50176]{1,0:T(8,128)(2,1)} reshape(bf16[27,3,16,7,448]{4,3,2,1,0:T(8,128)(2,1)} %fusion.50) | data formatting | bytes 16257024 | tf_op jit(solution)/shard_map/reshape | solution.py:179
  284.8 8.9 %fusion.103 = f32[81,96]{1,0:T(8,128)S(1)} fusion(bf16[81,50176]{1,0:T(8,128)(2,1)} %reshape.473, bf16[96,50176]{1,0:T(8,128)(2,1)} %reshape_squeeze.3), kind=kOutput, calls=%fused_computation.206 | convolution fusion | flops 780337152 | bytes 17793408 | tf_op jit(solution)/shard_map/dot_general | solution.py:189
  293.8 24.4 %all_to_all.51 = f32[16,81,96]{2,1,0:T(8,128)S(1)} all-to-all(f32[16,81,96]{2,1,0:T(8,128)S(1)} %broadcast_in_dim.70), channel_id=1, replica_groups=mesh['dp'=8,'space'=16] {'space'}, dimensions={0} | all-to-all | bytes 995328 | tf_op jit(solution)/shard_map/all_to_all | solution.py:54
  319.0 6.4 %all-to-all-start.3 = ((bf16[8,81,96]{2,1,0:T(8,128)(2,1)}), bf16[8,81,96]{2,1,0:T(8,128)(2,1)S(1)}, u32[]{:S(2)}, u32[]{:S(2)}) async-start(bf16[8,81,96]{2,1,0:T(8,128)(2,1)} %broadcast_in_dim.71), calls=%async_computation.3 | async-start | bytes 360448 | tf_op jit(solution)/shard_map/all_to_all | solution.py:54
  326.2 6.1 %all-to-all-done.3 = bf16[8,81,96]{2,1,0:T(8,128)(2,1)S(1)} async-done(((bf16[8,81,96]{2,1,0:T(8,128)(2,1)}), bf16[8,81,96]{2,1,0:T(8,128)(2,1)S(1)}, u32[]{:S(2)}, u32[]{:S(2)}) %all-to-all-start.3) | async-done | bytes 124448 | tf_op jit(solution)/shard_map/all_to_all | solution.py:54
  332.9 3.4 all-to-all-start.5
  337.3 5.7 %all-to-all-done.5 = bf16[8,24,384]{2,1,0:T(8,128)(2,1)S(1)} async-done(((bf16[8,24,384]{2,1,0:T(8,128)(2,1)}), bf16[8,24,384]{2,1,0:T(8,128)(2,1)S(1)}, u32[]{:S(2)}, u32[]{:S(2)}) %all-to-all-start.5) | async-done | bytes 147488 | tf_op jit(solution)/shard_map/all_to_all | solution.py:54
  343.7 3.8 all-to-all-start.4
  347.5 2.5 fusion.38
  350.1 5.3 %all-to-all-done.4 = bf16[8,24,1152]{2,1,0:T(8,128)(2,1)S(1)} async-done(((bf16[8,24,1152]{2,1,0:T(8,128)(2,1)}), bf16[8,24,1152]{2,1,0:T(8,128)(2,1)S(1)}, u32[]{:S(2)}, u32[]{:S(2)}) %all-to-all-start.4) | async-done | bytes 442400 | tf_op jit(solution)/shard_map/all_to_all | solution.py:54
  356.3 3.5 all-to-all-start.7
  359.9 10.0 %fusion.1 = bf16[96,50176]{1,0:T(8,128)(2,1)} fusion(bf16[81,50176]{1,0:T(8,128)(2,1)} %reshape.473, bf16[81,96]{1,0:T(8,128)(2,1)S(1)} %reshape.474), kind=kOutput, calls=%fused_computation.2 | convolution fusion | flops 785154048 | bytes 17777856 | tf_op jit(solution)/shard_map/dot_general | solution.py:185
  369.9 20.5 %convert_element_type.274 = bf16[1,96,16,7,448]{4,3,2,1,0:T(8,128)(2,1)} reshape(bf16[96,50176]{1,0:T(8,128)(2,1)} %fusion.1) | data formatting | bytes 19267584 | tf_op jit(solution)/shard_map/convert_element_type | solution.py:188
  390.4 12.1 %copy.141 = bf16[1,96,16,7,448]{4,2,3,1,0:T(8,128)(2,1)} copy(bf16[1,96,16,7,448]{4,3,2,1,0:T(8,128)(2,1)} %convert_element_type.274) | data formatting | bytes 19267584
  403.5 5.6 %all-to-all-start.6 = ((bf16[8,24,1536]{2,1,0:T(8,128)(2,1)}), bf16[8,24,1536]{2,1,0:T(8,128)(2,1)S(1)}, u32[]{:S(2)}, u32[]{:S(2)}) async-start(bf16[8,24,1536]{2,1,0:T(8,128)(2,1)} %broadcast_in_dim.74), calls=%async_computation.7 | async-start | bytes 1179648 | tf_op jit(solution)/shard_map/all_to_all | solution.py:54
  411.9 5.7 %all-to-all-done.6 = bf16[8,24,1536]{2,1,0:T(8,128)(2,1)S(1)} async-done(((bf16[8,24,1536]{2,1,0:T(8,128)(2,1)}), bf16[8,24,1536]{2,1,0:T(8,128)(2,1)S(1)}, u32[]{:S(2)}, u32[]{:S(2)}) %all-to-all-start.6) | async-done | bytes 589856 | tf_op jit(solution)/shard_map/all_to_all | solution.py:54
  (144 shorter events, 43.3 us)
Async XLA Ops:
  7.2 166.4 %copy-start = (bf16[384,1536]{1,0:T(8,128)(2,1)S(1)}, bf16[384,1536]{1,0:T(8,128)(2,1)}, u32[]{:S(2)}) copy-start(bf16[384,1536]{1,0:T(8,128)(2,1)} %param.20) | copy-start | bytes 3538948
  62.2 3.4 copy-start.3
  65.6 2.5 copy-start.2
  103.1 2.6 collective-permute-start
  104.4 6.5 %collective-permute-start.1 = (bf16[3,16,1,448]{3,1,2,0:T(8,128)(2,1)S(1)}, bf16[3,16,1,448]{3,1,2,0:T(8,128)(2,1)S(1)}, u32[]{:S(2)}, u32[]{:S(2)}) collective-permute-start(bf16[3,16,1,448]{3,1,2,0:T(8,128)(2,1)S(1)} %get-tuple-element.67), channel_id=1, source_target_pairs={{1,0},{2,1},{3,2},{4,3},{5,4},{6,5},{7,6},{8,7},{9,8},{10,9},{11,1... | collective-permute-start | bytes 129032 | tf_op jit(solution)/shard_map/ppermute | solution.py:12
  111.9 41.5 %all-to-all-start = ((bf16[3,16,7,448]{3,2,0,1:T(8,128)(2,1)}), bf16[3,16,7,448]{3,2,0,1:T(8,128)(2,1)S(1)}, u32[]{:S(2)}, u32[]{:S(2)}) async-start(bf16[3,16,7,448]{3,2,0,1:T(8,128)(2,1)} %copy.122), calls=%async_computation | async-start | bytes 786432 | tf_op jit(solution)/shard_map/all_to_all | solution.py:239
  161.0 5.6 %copy-start.23 = (bf16[256,384]{1,0:T(8,128)(2,1)S(1)}, bf16[256,384]{1,0:T(8,128)(2,1)}, u32[]{:S(2)}) copy-start(bf16[256,384]{1,0:T(8,128)(2,1)} %param.14) | copy-start | bytes 589828
  165.0 3.4 copy-start.6
  165.0 3.4 copy-start.25
  169.2 3.4 copy-start.16
  171.0 1.9 copy-start.21
  172.6 1.0 copy-start.26
  172.9 0.7 copy-start.14
  173.6 5.1 %copy-start.10 = (bf16[1,1,256,384]{3,2,1,0:T(8,128)(2,1)S(1)}, bf16[1,1,256,384]{3,2,1,0:T(8,128)(2,1)}, u32[]{:S(2)}) copy-start(bf16[1,1,256,384]{3,2,1,0:T(8,128)(2,1)} %param.13) | copy-start | bytes 589828
  173.6 5.1 %copy-start.20 = (bf16[1536,384]{1,0:T(8,128)(2,1)S(1)}, bf16[1536,384]{1,0:T(8,128)(2,1)}, u32[]{:S(2)}) copy-start(bf16[1536,384]{1,0:T(8,128)(2,1)} %param.21) | copy-start | bytes 3538948
  182.1 1.1 copy-start.17
  187.3 1.6 copy-start.7
  187.3 2.8 copy-start.5
  191.6 2.5 copy-start.8
  195.6 2.6 copy-start.18
  195.6 2.9 copy-start.13
  202.9 14.3 %copy-start.15 = (bf16[6,64,256]{2,1,0:T(8,128)(2,1)S(1)}, bf16[6,64,256]{2,1,0:T(8,128)(2,1)}, u32[]{:S(2)}) copy-start(bf16[6,64,256]{2,1,0:T(8,128)(2,1)} %copy-done.14) | copy-start | bytes 589828
  209.7 9.1 %copy-start.11 = (bf16[256,1536]{1,0:T(8,128)(2,1)S(1)}, bf16[256,1536]{1,0:T(8,128)(2,1)}, u32[]{:S(2)}) copy-start(bf16[256,1536]{1,0:T(8,128)(2,1)} %get-tuple-element.53) | copy-start | bytes 2359300
  209.7 19.3 %all-to-all-start.1 = ((bf16[3,1,112,448]{3,0,1,2:T(4,128)(2,1)}), bf16[3,1,112,448]{3,0,1,2:T(4,128)(2,1)}, u32[]{:S(2)}, u32[]{:S(2)}) async-start(bf16[3,1,112,448]{3,0,1,2:T(4,128)(2,1)} %copy.132), calls=%async_computation.1 | async-start | bytes 917504 | tf_op jit(solution)/shard_map/all_to_all | solution.py:241
  217.2 108.2 %reduce-scatter.2.cloned.1.call-start = ((), (), s32[]{:S(2)}) async-start(), calls=%async_computation.9 | async-start | bytes 3760128 | tf_op jit(solution)/shard_map/reduce_scatter | solution.py:44
  220.4 13.1 %copy-start.4 = (bf16[16,36864]{1,0:T(8,128)(2,1)S(1)}, bf16[16,36864]{1,0:T(8,128)(2,1)}, u32[]{:S(2)}) copy-start(bf16[16,36864]{1,0:T(8,128)(2,1)} %convert_element_type.288) | copy-start | bytes 3538948
  220.4 13.1 %copy-start.19 = (bf16[16,9216]{1,0:T(8,128)(2,1)S(1)}, bf16[16,9216]{1,0:T(8,128)(2,1)}, u32[]{:S(2)}) copy-start(bf16[16,9216]{1,0:T(8,128)(2,1)} %convert_element_type.284) | copy-start | bytes 884740
  228.9 4.6 %copy-start.9 = (bf16[16,27648]{1,0:T(8,128)(2,1)S(1)}, bf16[16,27648]{1,0:T(8,128)(2,1)}, u32[]{:S(2)}) copy-start(bf16[16,27648]{1,0:T(8,128)(2,1)} %convert_element_type.280) | copy-start | bytes 2654212
  230.9 8.9 %collective-permute-start.2 = (bf16[3,16,1,448]{3,2,1,0:T(2,128)(2,1)}, bf16[3,16,1,448]{3,2,1,0:T(2,128)(2,1)S(1)}, u32[]{:S(2)}, u32[]{:S(2)}) collective-permute-start(bf16[3,16,1,448]{3,2,1,0:T(2,128)(2,1)} %get-tuple-element.68), channel_id=1, source_target_pairs={{0,1},{1,2},{2,3},{3,4},{4,5},{5,6},{6,7},{7,8},{8,9},{9,10},{10,1... | collective-permute-start | bytes 129032 | tf_op jit(solution)/shard_map/ppermute | solution.py:23
  232.2 7.6 %collective-permute-start.3 = (bf16[3,16,1,448]{3,2,1,0:T(2,128)(2,1)}, bf16[3,16,1,448]{3,2,1,0:T(2,128)(2,1)}, u32[]{:S(2)}, u32[]{:S(2)}) collective-permute-start(bf16[3,16,1,448]{3,2,1,0:T(2,128)(2,1)} %get-tuple-element.69), channel_id=1, source_target_pairs={{1,0},{2,1},{3,2},{4,3},{5,4},{6,5},{7,6},{8,7},{9,8},{10,9},{11,1... | collective-permute-start | bytes 129032 | tf_op jit(solution)/shard_map/ppermute | solution.py:25
  293.8 42.5 %copy-start.24 = (bf16[3,3,3,3,96]{4,3,2,1,0:T(4,128)(2,1)S(1)}, bf16[3,3,3,3,96]{4,3,2,1,0:T(4,128)(2,1)}, u32[]{:S(2)}) copy-start(bf16[3,3,3,3,96]{4,3,2,1,0:T(4,128)(2,1)} %param.12) | copy-start | bytes 46660
  318.3 29.3 %copy-start.12 = (bf16[256,1536]{1,0:T(8,128)(2,1)S(1)}, bf16[256,1536]{1,0:T(8,128)(2,1)}, u32[]{:S(2)}) copy-start(bf16[256,1536]{1,0:T(8,128)(2,1)} %get-tuple-element.53) | copy-start | bytes 2359300
  319.0 13.2 %all-to-all-start.3 = ((bf16[8,81,96]{2,1,0:T(8,128)(2,1)}), bf16[8,81,96]{2,1,0:T(8,128)(2,1)S(1)}, u32[]{:S(2)}, u32[]{:S(2)}) async-start(bf16[8,81,96]{2,1,0:T(8,128)(2,1)} %broadcast_in_dim.71), calls=%async_computation.3 | async-start | bytes 360448 | tf_op jit(solution)/shard_map/all_to_all | solution.py:54
  332.9 10.0 %all-to-all-start.5 = ((bf16[8,24,384]{2,1,0:T(8,128)(2,1)}), bf16[8,24,384]{2,1,0:T(8,128)(2,1)S(1)}, u32[]{:S(2)}, u32[]{:S(2)}) async-start(bf16[8,24,384]{2,1,0:T(8,128)(2,1)} %broadcast_in_dim.73), calls=%async_computation.6 | async-start | bytes 294912 | tf_op jit(solution)/shard_map/all_to_all | solution.py:54
  343.7 6.4 %copy-start.22 = (bf16[864,128]{1,0:T(8,128)(2,1)S(1)}, bf16[864,128]{1,0:T(8,128)(2,1)}, u32[]{:S(2)}) copy-start(bf16[864,128]{1,0:T(8,128)(2,1)} %reduce-scatter.2.cloned.1.call-done) | copy-start | bytes 663556
  343.7 11.7 %all-to-all-start.4 = ((bf16[8,24,1152]{2,1,0:T(8,128)(2,1)}), bf16[8,24,1152]{2,1,0:T(8,128)(2,1)S(1)}, u32[]{:S(2)}, u32[]{:S(2)}) async-start(bf16[8,24,1152]{2,1,0:T(8,128)(2,1)} %broadcast_in_dim.72), calls=%async_computation.5 | async-start | bytes 884736 | tf_op jit(solution)/shard_map/all_to_all | solution.py:54
  356.3 46.3 %all-to-all-start.7 = ((bf16[8,96,384]{2,1,0:T(8,128)(2,1)}), bf16[8,96,384]{2,1,0:T(8,128)(2,1)S(1)}, u32[]{:S(2)}, u32[]{:S(2)}) async-start(bf16[8,96,384]{2,1,0:T(8,128)(2,1)} %broadcast_in_dim.75), calls=%async_computation.8 | async-start | bytes 1179648 | tf_op jit(solution)/shard_map/all_to_all | solution.py:54
  402.6 15.8 %copy-start.1 = (bf16[384,1536]{1,0:T(8,128)(2,1)S(1)}, bf16[384,1536]{1,0:T(8,128)(2,1)}, u32[]{:S(2)}) copy-start(bf16[384,1536]{1,0:T(8,128)(2,1)} %param.20) | copy-start | bytes 3538948
  403.5 14.2 %all-to-all-start.6 = ((bf16[8,24,1536]{2,1,0:T(8,128)(2,1)}), bf16[8,24,1536]{2,1,0:T(8,128)(2,1)S(1)}, u32[]{:S(2)}, u32[]{:S(2)}) async-start(bf16[8,24,1536]{2,1,0:T(8,128)(2,1)} %broadcast_in_dim.74), calls=%async_computation.7 | async-start | bytes 1179648 | tf_op jit(solution)/shard_map/all_to_all | solution.py:54
Sparse Core Ops, SparseCore 0:
  239.9 83.3 reduce-scatter.1
where the time goes:
time: 432 us; the launch traced here: 425 us
  local copies, waits for them, and re-layouts  185 us (43%)
  matrix products  81.6 us (19%)
  starting transfers between devices  45.5 us (11%)
  other arithmetic  39.9 us (9%)
  waiting for transfers between devices  34.7 us (8%)
  blocking collectives  24.4 us (6%)
  between operations  14.9 us (3%)
    unnamed x85, local copies, waits for them, and re-layouts  60.9 us
    dot_general x1, matrix products, project_taps(): lax.dot_general(tap_matrix, feature_tile, (((1,), (0,)), ((), ())), prefe...  37.1 us
    all_to_all x1, blocking collectives, from_everyone(): return lax.all_to_all(copies, axis, split_axis=0, concat_axis=0, tiled=True)  24.4 us
    add x2, other arithmetic, time_parts(): total = piece if total is None else total + piece  23.5 us
    all_to_all x5, starting transfers between devices, from_everyone(): return lax.all_to_all(copies, axis, split_axis=0, concat_axis=0, tiled=True)  22.7 us
    all_to_all x5, waiting for transfers between devices, from_everyone(): return lax.all_to_all(copies, axis, split_axis=0, concat_axis=0, tiled=True)  22.7 us
    convert_element_type x1, local copies, waits for them, and re-layouts, conv_backward(): feature_grad = feature_grad.reshape(feature_tile.shape).astype(jnp.bfloat16)  20.5 us
    another operation x1, local copies, waits for them, and re-layouts, conv_backward(): flat = feature_tile.reshape(channels, -1)  17.8 us
  transfers between devices with their start and end apart: 12, of which 6 were waited for; matrix products, arithmetic and copies ran while one was open for 35% of the time, Pallas kernels for 0%

commit v1 on v0

v1 whole, which is shorter than its diff:
```python
import functools

import jax
import jax.numpy as jnp
from jax import lax
from jax.experimental import pallas as pl
from jax.experimental.pallas import tpu as pltpu
from jax.sharding import PartitionSpec as P

HEADS = 6
BF = jnp.bfloat16
F32 = jnp.float32
NN = (((1,), (0,)), ((), ()))
NT = (((1,), (1,)), ((), ()))
TN = (((0,), (0,)), ((), ()))


def dot(a, b, dims=NN):
    return lax.dot_general(a, b, dims, preferred_element_type=F32)


def iota(shape, dim):
    return lax.broadcasted_iota(jnp.int32, shape, dim)


def one_hot(cond):
    return jnp.where(cond, 1.0, 0.0).astype(BF)


def group_source(group):
    return (2 - group // 9) * 9 + group % 9


def band(w81):
    spread = one_hot(iota((96, 1536), 1) // 16 == iota((96, 1536), 0))
    row = iota((432, 81), 0)
    source = group_source(row // 16)
    lag = iota((432, 1536), 1) % 16 - iota((432, 1536), 0) % 16 + 2
    total = None
    for a in range(3):
        picked = dot(one_hot(iota((432, 81), 1) == source + 27 * a), w81).astype(BF)
        piece = jnp.where(lag == a, dot(picked, spread), 0.0)
        total = piece if total is None else total + piece
    return total.astype(BF)


def band_transposed(w81):
    spread = one_hot(iota((1536, 96), 0) // 16 == iota((1536, 96), 1))
    source = group_source(iota((81, 432), 1) // 16)
    lag = iota((1536, 432), 0) % 16 - iota((1536, 432), 1) % 16 + 2
    total = None
    for a in range(3):
        picked = dot(w81, one_hot(iota((81, 432), 0) == source + 27 * a), TN).astype(BF)
        piece = jnp.where(lag == a, dot(spread, picked), 0.0)
        total = piece if total is None else total + piece
    return total.astype(BF)


def conv_forward_kernel(w_ref, x_ref, out_ref, band_ref, acc_ref, rows_ref):
    step = pl.program_id(0)

    @pl.when(step == 0)
    def _():
        band_ref[...] = band(w_ref[...])
        acc_ref[...] = jnp.zeros_like(acc_ref)
        rows_ref[...] = jnp.zeros_like(rows_ref)

    x = x_ref[:, 0].reshape(1536, 448)
    at = pl.ds(pl.multiple_of(step * 144, 16), 432)
    acc_ref[at, :448] += dot(band_ref[...], x)

    @pl.when(step == 6)
    def _():
        for row in range(9):
            taps = acc_ref[row * 144 : (row + 1) * 144, :]
            out = pltpu.roll(taps[0:48], 1, 1) + taps[48:96] + pltpu.roll(taps[96:144], 511, 1)
            for o in range(3):
                for t in range(4):
                    rows_ref[t, pl.ds(o * 9 + row, 16, stride=32), :] = out[
                        o * 16 : (o + 1) * 16, t * 128 : t * 128 + 128
                    ]
        for t in range(3):
            out_ref[:, t * 128 : t * 128 + 128] = rows_ref[t].astype(BF)
        out_ref[:, 384:448] = rows_ref[3, :, :64].astype(BF)


def conv_forward(features, w81):
    return pl.pallas_call(
        conv_forward_kernel,
        grid=(7,),
        out_shape=jax.ShapeDtypeStruct((512, 448), BF),
        in_specs=[
            pl.BlockSpec((81, 96), lambda h: (0, 0)),
            pl.BlockSpec((96, 1, 16, 448), lambda h: (0, h, 0, 0)),
        ],
        out_specs=pl.BlockSpec((512, 448), lambda h: (0, 0)),
        scratch_shapes=[
            pltpu.VMEM((432, 1536), BF),
            pltpu.VMEM((1296, 512), F32),
            pltpu.VMEM((4, 512, 128), F32),
        ],
        name="conv_forward",
    )(w81, features)


def conv_backward_kernel(w_ref, v_ref, x_ref, fg_ref, conv_ref, band_ref, pg_ref, rows_ref, g_ref):
    step = pl.program_id(0)

    @pl.when(step == 0)
    def _():
        band_ref[...] = band_transposed(w_ref[...])
        for t in range(3):
            rows_ref[t] = v_ref[:, t * 128 : t * 128 + 128].astype(F32)
        rows_ref[3] = jnp.zeros((512, 128), F32)
        rows_ref[3, :, :64] = v_ref[:, 384:448].astype(F32)
        for row in range(9):
            for o in range(3):
                v = jnp.concatenate(
                    [rows_ref[t, pl.ds(o * 9 + row, 16, stride=32), :] for t in range(4)], axis=1
                )
                for e in range(3):
                    moved = v if e == 1 else pltpu.roll(v, 511 if e == 0 else 1, 1)
                    at = (row * 9 + e * 3 + o) * 16
                    pg_ref[at : at + 16, :] = moved.astype(BF)
        g_ref[...] = jnp.zeros_like(g_ref)

    x = x_ref[:, 0].reshape(1536, 448)
    pg = pg_ref[pl.ds(pl.multiple_of(step * 144, 16), 432), :448]
    fg_ref[:, 0] = dot(band_ref[...], pg).astype(BF).reshape(96, 16, 448)
    g_ref[...] += dot(pg, x, NT)

    @pl.when(step == 6)
    def _():
        spread = one_hot(iota((1536, 96), 0) // 16 == iota((1536, 96), 1))
        lag = iota((16, 1536), 1) % 16 - iota((16, 1536), 0) + 2
        for a in range(3):
            keep = lag == a
            sums = [
                jnp.sum(jnp.where(keep, g_ref[g * 16 : (g + 1) * 16, :], 0.0), axis=0, keepdims=True)
                for g in range(27)
            ]
            sums = [sums[(2 - b) * 9 + eo] for b in range(3) for eo in range(9)]
            total = jnp.concatenate(sums, axis=0)
            high = total.astype(BF)
            rest = total - high.astype(F32)
            middle = rest.astype(BF)
            conv_ref[a * 27 : (a + 1) * 27, :] = dot(high, spread) + dot(middle, spread)


def conv_backward(features, w81, grad_rows):
    return pl.pallas_call(
        conv_backward_kernel,
        grid=(7,),
        out_shape=(
            jax.ShapeDtypeStruct((96, 7, 16, 448), BF),
            jax.ShapeDtypeStruct((81, 96), F32),
        ),
        in_specs=[
            pl.BlockSpec((81, 96), lambda h: (0, 0)),
            pl.BlockSpec((512, 448), lambda h: (0, 0)),
            pl.BlockSpec((96, 1, 16, 448), lambda h: (0, h, 0, 0)),
        ],
        out_specs=(
            pl.BlockSpec((96, 1, 16, 448), lambda h: (0, h, 0, 0)),
            pl.BlockSpec((81, 96), lambda h: (0, 0)),
        ),
        scratch_shapes=[
            pltpu.VMEM((1536, 432), BF),
            pltpu.VMEM((1296, 512), BF),
            pltpu.VMEM((4, 512, 128), F32),
            pltpu.VMEM((432, 1536), F32),
        ],
        name="conv_backward",
    )(w81, grad_rows, features)


def patch_matrix(patch_weight):
    row = iota((896, 588), 0)
    tile_row = row % 32
    colour, height = tile_row // 9, tile_row % 9
    piece = row // 32
    half, column = piece // 14, piece % 14
    line = (7 * half + height + 13) % 14
    source = colour * 196 + line * 14 + column
    return dot(one_hot((iota((896, 588), 1) == source) & (tile_row < 27)), patch_weight).astype(BF)


def norm_forward(values, gain):
    centered = values - jnp.mean(values, axis=-1, keepdims=True)
    scale = lax.rsqrt(jnp.mean(centered * centered, axis=-1, keepdims=True) + 1e-06)
    unit = centered * scale
    return unit, scale, (unit * gain).astype(BF)


def norm_backward(unit, scale, gain, grad):
    grad = grad * gain
    return scale * (
        grad
        - jnp.mean(grad, axis=-1, keepdims=True)
        - unit * jnp.mean(grad * unit, axis=-1, keepdims=True)
    )


def frame_kernel(
    z_ref, g_ref, pos_ref, pw_ref, n1_ref, wqkv_ref, wproj_ref, n2_ref, w1_ref, w2_ref,
    out_ref, dz_ref, dqkv_ref, dproj_ref, d1_ref, d2_ref,
    wp_ref, a_ref, r_ref, pk_ref, dpk_ref, prob_ref,
):
    wp_ref[...] = patch_matrix(pw_ref[...])
    z = z_ref[...].astype(F32)
    place = iota((512, 448), 0)
    tile, tile_row = place // 32, place % 32
    height = tile_row % 9
    used = tile_row < 27
    above = pltpu.roll(z, 25, 0)
    below = pltpu.roll(z, 487, 0)
    z = z + jnp.where((height == 1) & (tile > 0), above, 0.0)
    z = z + jnp.where((height == 7) & (tile < 15), below, 0.0)
    z = jnp.where(used & (height > 0) & (height < 8), z, 0.0).astype(BF)
    pick = iota((448, 448), 0)
    permute = one_hot(iota((448, 448), 1) == (pick % 32) * 14 + pick // 32)
    turned = dot(permute, z, NT)
    for tile_at in range(16):
        for column in range(14):
            at = ((tile_at % 2) * 14 + column) * 32
            a_ref[tile_at // 2 * 32 : tile_at // 2 * 32 + 32, at : at + 32] = turned[
                column * 32 : column * 32 + 32, tile_at * 32 : tile_at * 32 + 32
            ]
    embedded = dot(a_ref[...].astype(BF), wp_ref[...]) + pos_ref[...].astype(F32)
    gain1, gain2 = n1_ref[...], n2_ref[...]
    unit1, scale1, normed = norm_forward(embedded, gain1)
    pk_ref[...] = dot(normed, wqkv_ref[...]).astype(BF)
    left = iota((256, 128), 1) < 64
    zero = jnp.zeros((256, 128), BF)
    attended = []
    for pair in range(3):
        q = pk_ref[:, pair * 128 : pair * 128 + 128]
        k = pk_ref[:, 384 + pair * 128 : 384 + pair * 128 + 128]
        v = pk_ref[:, 768 + pair * 128 : 768 + pair * 128 + 128]
        both = []
        for side in range(2):
            mine = left if side == 0 else ~left
            s = dot(jnp.where(mine, q, zero), k, NT) * 0.125
            s = jnp.exp(s - jnp.max(s, axis=-1, keepdims=True))
            s = s / jnp.sum(s, axis=-1, keepdims=True)
            prob_ref[pair * 2 + side] = s
            both.append(dot(s.astype(BF), v))
        attended.append(jnp.where(left, both[0], both[1]).astype(BF))
    attended = jnp.concatenate(attended, axis=1)
    residual = embedded + dot(attended, wproj_ref[...])
    unit2, scale2, normed2 = norm_forward(residual, gain2)
    g = g_ref[...]
    out = residual
    dnormed2 = jnp.zeros((256, 384), F32)
    for part in range(3):
        cols = slice(part * 512, part * 512 + 512)
        pre = dot(normed2, w1_ref[:, cols])
        cdf = 0.5 + 0.5 * lax.erf(pre * 0.7071067811865476)
        hidden = (pre * cdf).astype(BF)
        out = out + dot(hidden, w2_ref[cols, :])
        d2_ref[cols, :] = dot(hidden, g, TN).astype(BF)
        dhidden = dot(g, w2_ref[cols, :], NT).astype(BF).astype(F32)
        slope = cdf + pre * (0.3989422804014327 * jnp.exp(-0.5 * pre * pre))
        dpre = (dhidden * slope).astype(BF)
        d1_ref[:, cols] = dot(normed2, dpre, TN).astype(BF)
        dnormed2 = dnormed2 + dot(dpre, w1_ref[:, cols], NT)
    out_ref[...] = out.astype(BF)
    dnormed2 = dnormed2.astype(BF).astype(F32)
    dres = g.astype(F32) + norm_backward(unit2, scale2, gain2, dnormed2)
    dres_bf = dres.astype(BF)
    dproj_ref[...] = dot(attended, dres_bf, TN).astype(BF)
    datt = dot(dres_bf, wproj_ref[...], NT).astype(BF)
    for pair in range(3):
        q = pk_ref[:, pair * 128 : pair * 128 + 128]
        k = pk_ref[:, 384 + pair * 128 : 384 + pair * 128 + 128]
        v = pk_ref[:, 768 + pair * 128 : 768 + pair * 128 + 128]
        da = datt[:, pair * 128 : pair * 128 + 128]
        dq, dk, dv = [], [], []
        for side in range(2):
            mine = left if side == 0 else ~left
            p = prob_ref[pair * 2 + side]
            dp = dot(jnp.where(mine, da, zero), v, NT).astype(BF).astype(F32)
            dv.append(dot(p.astype(BF), da, TN))
            ds = p * (dp - jnp.sum(dp * p, axis=-1, keepdims=True)) * 0.125
            ds = ds.astype(BF)
            dq.append(dot(ds, k))
            dk.append(dot(ds, q, TN))
        dpk_ref[:, pair * 128 : pair * 128 + 128] = jnp.where(left, dq[0], dq[1]).astype(BF)
        dpk_ref[:, 384 + pair * 128 : 384 + pair * 128 + 128] = jnp.where(left, dk[0], dk[1]).astype(BF)
        dpk_ref[:, 768 + pair * 128 : 768 + pair * 128 + 128] = jnp.where(left, dv[0], dv[1]).astype(BF)
    dpk = dpk_ref[...]
    dqkv_ref[...] = dot(normed, dpk, TN).astype(BF)
    dnormed = dot(dpk, wqkv_ref[...], NT).astype(BF).astype(F32)
    demb = dres + norm_backward(unit1, scale1, gain1, dnormed)
    a_ref[...] = dot(demb.astype(BF), wp_ref[...], NT)
    for tile_at in range(16):
        for column in range(14):
            at = ((tile_at % 2) * 14 + column) * 32
            r_ref[column * 32 : column * 32 + 32, tile_at * 32 : tile_at * 32 + 32] = a_ref[
                tile_at // 2 * 32 : tile_at // 2 * 32 + 32, at : at + 32
            ]
    dz = dot(r_ref[...].astype(BF), permute, TN)
    odd = tile % 2 == 1
    nothing = jnp.zeros((64, 448), F32)
    above = jnp.concatenate([nothing, dz[:448]], axis=0)
    below = jnp.concatenate([dz[64:], nothing], axis=0)
    dz = jnp.where((height == 0) & ~odd, above, dz)
    dz = jnp.where((height == 8) & odd, below, dz)
    dz_ref[...] = dz.astype(BF)


def frame_step(z, g, pos, pw, n1, wqkv, wproj, n2, w1, w2):
    return pl.pallas_call(
        frame_kernel,
        out_shape=(
            jax.ShapeDtypeStruct((256, 384), BF),
            jax.ShapeDtypeStruct((512, 448), BF),
            jax.ShapeDtypeStruct((384, 1152), BF),
            jax.ShapeDtypeStruct((384, 384), BF),
            jax.ShapeDtypeStruct((384, 1536), BF),
            jax.ShapeDtypeStruct((1536, 384), BF),
        ),
        scratch_shapes=[
            pltpu.VMEM((896, 384), BF),
            pltpu.VMEM((256, 896), F32),
            pltpu.VMEM((448, 512), F32),
            pltpu.VMEM((256, 1152), BF),
            pltpu.VMEM((256, 1152), BF),
            pltpu.VMEM((6, 256, 256), F32),
        ],
        name="frame_step",
    )(z, g, pos, pw, n1, wqkv, wproj, n2, w1, w2)


def in_blocks(x, length):
    return x.reshape(length, x.shape[0] // length, *x.shape[1:])


def one_scatter(arrays, axis):
    length = lax.axis_size(axis)
    blocks = [in_blocks(a, length) for a in arrays]
    lines = jnp.concatenate([b.reshape(length, -1, 128) for b in blocks], axis=1).reshape(-1, 128)
    mine = lax.psum_scatter(lines, axis, tiled=True)
    return mine, blocks


def from_everyone(x, axis):
    copies = jnp.broadcast_to(x, (lax.axis_size(axis), *x.shape))
    return lax.all_to_all(copies, axis, split_axis=0, concat_axis=0, tiled=True)


def shards(
    features, conv_weight, out_grad, pos_embed, patch_weight, norm1, qkv_weight, proj_weight,
    norm2, fc1_weight, fc2_weight,
):
    tile = features[0].transpose(0, 2, 1, 3)
    w81 = conv_weight.reshape(81, 96)
    rows = conv_forward(tile, w81).reshape(16, 32, 448)
    rows = lax.all_to_all(rows, "space", split_axis=0, concat_axis=0, tiled=True)
    block_out, grad_rows, dqkv, dproj, d1, d2 = frame_step(
        rows.reshape(512, 448), out_grad[0, 0], pos_embed, patch_weight, norm1[None],
        qkv_weight, proj_weight, norm2[None], fc1_weight, fc2_weight,
    )
    grad_rows = lax.all_to_all(
        grad_rows.reshape(16, 32, 448), "space", split_axis=0, concat_axis=0, tiled=True
    )
    feature_grad, conv_part = conv_backward(tile, w81, grad_rows.reshape(512, 448))
    mine, blocks = one_scatter((dqkv, dproj, d1, d2), "space")
    conv_space = from_everyone(conv_part, "space").sum(axis=0)
    total = from_everyone(mine, "dp").astype(F32).sum(axis=0)
    conv_total = from_everyone(conv_space.astype(BF), "dp").astype(F32).sum(axis=0)
    shares, at = [], 0
    for b in blocks:
        part = b[0]
        lines = part.size // 128
        shares.append(total[at : at + lines].reshape(part.shape))
        at += lines
    return (
        block_out[None, None],
        feature_grad.transpose(0, 2, 1, 3)[None],
        conv_total.reshape(conv_weight.shape),
        *shares,
    )


def solution(mesh):
    placed = (
        P("dp", None, None, "space", None),
        P(),
        P("dp", "space", None, None),
        *([P()] * 8),
    )
    return jax.shard_map(
        shards,
        mesh=mesh,
        in_specs=placed,
        out_specs=(
            P("dp", "space", None, None),
            P("dp", None, None, "space", None),
            P(),
            *([P("space", None)] * 4),
        ),
        check_vma=False,
    )
```

time: 432 us -> 186 us (0.43); the launches traced: 425 us -> 185 us
  local copies, waits for them, and re-layouts: 185 us -> 19.3 us
  matrix products: 81.6 us -> 0 us
  Pallas kernels: 0 us -> 50.1 us
  other arithmetic: 39.9 us -> 2.3 us
  starting transfers between devices: 45.5 us -> 11.8 us
  blocking collectives: 24.4 us -> 45 us
  waiting for transfers between devices: 34.7 us -> 42.5 us
    dot_general x22 -> x0, matrix products: 79.8 us -> none  [the longest x1 37.1 us: project_taps(): lax.dot_general(tap_matrix, feature_tile, (((1,), (0,)), ((), ())), prefe...]
    unnamed x85 -> x8, local copies, waits for them, and re-layouts: 60.9 us -> 1.82 us
    pallas_call x0 -> x3, Pallas kernels: none -> 50.1 us  [the longest x1 20.7 us: conv_backward(): pl.pallas_call(conv_backward_kernel, grid=(7,), out_shape=(jax.ShapeDtype...]
    convert_element_type x11 -> x0, local copies, waits for them, and re-layouts: 32.8 us -> none  [the longest x1 20.5 us: conv_backward(): feature_grad = feature_grad.reshape(feature_tile.shape).astype(jnp.bfloat16)]
    reshape x11 -> x5, local copies, waits for them, and re-layouts: 31.6 us -> 4.05 us  [the longest x4 2.67 us: shards(): shares.append(total[at:at + lines].reshape(part.shape))]
    add x3 -> x0, other arithmetic: 27 us -> none  [the longest x2 23.5 us: time_parts(): total = piece if total is None else total + piece]
    slice x6 -> x3, local copies, waits for them, and re-layouts: 19.5 us -> 0.04 us  [shards(): shares.append(total[at:at + lines].reshape(part.shape))]
    all_to_all x5 -> x1, starting transfers between devices: 22.7 us -> 4.46 us  [from_everyone(): return lax.all_to_all(copies, axis, split_axis=0, concat_axis=0, tiled=True)]
  transfers between devices with their start and end apart: 12 -> 3, of which waited for: 6 -> 3; matrix products, arithmetic and copies ran while one was open for 35% -> 2% of each run, Pallas kernels for 0% -> 11%
where the time goes in v1:
time: 186 us; the launch traced here: 185 us
  Pallas kernels  50.1 us (27%)
  blocking collectives  45 us (24%)
  waiting for transfers between devices  42.5 us (23%)
  local copies, waits for them, and re-layouts  19.3 us (10%)
  between operations  14.1 us (8%)
  starting transfers between devices  11.8 us (6%)
  other arithmetic  2.3 us (1%)
    all_to_all x2, blocking collectives, from_everyone(): return lax.all_to_all(copies, axis, split_axis=0, concat_axis=0, tiled=True)  29.4 us
    pallas_call x1, Pallas kernels, conv_backward(): pl.pallas_call(conv_backward_kernel, grid=(7,), out_shape=(jax.ShapeDtype...  20.7 us
    all_to_all x1, waiting for transfers between devices, from_everyone(): return lax.all_to_all(copies, axis, split_axis=0, concat_axis=0, tiled=True)  20 us
    pallas_call x1, Pallas kernels, frame_step(): pl.pallas_call(frame_kernel, out_shape=(jax.ShapeDtypeStruct((256, 384),...  16.2 us
    all_to_all x1, blocking collectives, shards(): lax.all_to_all(grad_rows.reshape(16, 32, 448), 'space', split_axis=0, con...  15.6 us
    pallas_call x1, Pallas kernels, conv_forward(): pl.pallas_call(conv_forward_kernel, grid=(7,), out_shape=jax.ShapeDtypeSt...  13.2 us
    reduce_scatter x1, waiting for transfers between devices, one_scatter(): mine = lax.psum_scatter(lines, axis, tiled=True)  11.5 us
    all_to_all x1, waiting for transfers between devices, shards(): lax.all_to_all(rows, 'space', split_axis=0, concat_axis=0, tiled=True)  11 us
  transfers between devices with their start and end apart: 3, of which 3 were waited for; matrix products, arithmetic and copies ran while one was open for 2% of the time, Pallas kernels for 11%

profile of v1, /device:TPU:0, one launch (start us, length us, event | category | flops | bytes accessed | tf_op | source)
XLA Modules:
  0.0 185.2 jit_solution(17900690498421716372)
XLA Ops:
  7.2 1.4 reshape.47.w_ref
  8.5 0.0 copy-start.2
  8.5 0.0 copy-start.3
  8.5 13.2 %conv_forward.1 = bf16[512,448]{1,0:T(8,128)(2,1)} custom-call(bf16[81,96]{1,0:T(8,128)(2,1)} %reshape.47.w_ref, bf16[96,7,16,448]{3,2,1,0:T(8,128)(2,1)} %bitcast.13), custom_call_target="tpu_custom_call" | custom-call | tf_op jit(solution)/shard_map/conv_forward/pallas_call | solution.py:88
  21.8 7.1 %all-to-all-start = ((bf16[16,32,448]{2,1,0:T(8,128)(2,1)}), bf16[16,32,448]{2,1,0:T(8,128)(2,1)S(1)}, u32[]{:S(2)}, u32[]{:S(2)}) async-start(bf16[16,32,448]{2,1,0:T(8,128)(2,1)} %bitcast.17), calls=%async_computation | async-start | bytes 1048576 | tf_op jit(solution)/shard_map/all_to_all | solution.py:359
  28.9 0.2 reduce-scatter.2.cloned.1.call-start
  29.1 0.0 copy-done.2
  29.1 0.6 broadcast_in_dim.21.n1_ref
  29.7 0.0 copy-done.3
  29.7 0.6 broadcast_in_dim.22.n2_ref
  30.3 11.0 %all-to-all-done = bf16[16,32,448]{2,1,0:T(8,128)(2,1)S(1)} async-done(((bf16[16,32,448]{2,1,0:T(8,128)(2,1)}), bf16[16,32,448]{2,1,0:T(8,128)(2,1)S(1)}, u32[]{:S(2)}, u32[]{:S(2)}) %all-to-all-start) | async-done | bytes 458784 | tf_op jit(solution)/shard_map/all_to_all | solution.py:359
  41.2 0.0 copy-start
  41.2 0.8 copy-done
  42.0 16.2 %frame_step.1 = (bf16[256,384]{1,0:T(8,128)(2,1)}, bf16[512,448]{1,0:T(8,128)(2,1)}, bf16[384,1152]{1,0:T(8,128)(2,1)}, bf16[384,384]{1,0:T(8,128)(2,1)}, bf16[3...) custom-call(bf16[512,448]{1,0:T(8,128)(2,1)} %bitcast.16, bf16[256,384]{1,0:T(8,128)(2,1)} %bitcast.20, ...), custom_call_target="tpu_custom_call" | custom-call | tf_op jit(solution)/shard_map/frame_step/pallas_call | solution.py:313
  58.3 1.1 reshape_reshape.13
  59.4 2.3 %reshape_reshape.12 = bf16[16,216,128]{2,1,0:T(8,128)(2,1)S(1)} reshape(bf16[384,1152]{1,0:T(8,128)(2,1)} %get-tuple-element.19) | data formatting | bytes 1769472 | tf_op jit(solution)/shard_map/reshape;reshape | solution.py:342
  61.7 2.8 %reshape_reshape.14 = bf16[16,288,128]{2,1,0:T(8,128)(2,1)S(1)} reshape(bf16[384,1536]{1,0:T(8,128)(2,1)} %get-tuple-element.21) | data formatting | bytes 2359296 | tf_op jit(solution)/shard_map/reshape;reshape | solution.py:342
  64.4 2.3 %reshape_reshape.15 = bf16[16,288,128]{2,1,0:T(8,128)(2,1)S(1)} reshape(bf16[1536,384]{1,0:T(8,128)(2,1)} %get-tuple-element.22) | data formatting | bytes 2359296 | tf_op jit(solution)/shard_map/reshape;reshape | solution.py:342
  66.7 1.9 %pad_maximum_fusion = bf16[16,864,128]{2,1,0:T(8,128)(2,1)} fusion(bf16[16,288,128]{2,1,0:T(8,128)(2,1)S(1)} %reshape_reshape.15, bf16[16,288,128]{2,1,0:T(8,128)(2,1)S(1)} %reshape_reshape.14, bf16[16,72,128]{2,1,0:T(8,128)(2,1)S(1)} %reshape_reshape.13, bf16[16,216,128]{2,1,0:T(8,128)(2,1)S(1)} %reshape_reshape.12), kind=kLoop, calls=%fused_computation | loop fusion | flops 14155776 | bytes 7077888 | tf_op jit(solution)/shard_map/concatenate | solution.py:342
  68.6 0.0 copy-start.1
  68.6 0.0 reduce-scatter.2.cloned.1.call-update
  68.6 1.0 copy-done.1
  69.7 15.6 %all_to_all.25 = bf16[16,32,448]{2,1,0:T(8,128)(2,1)} all-to-all(bf16[16,32,448]{2,1,0:T(8,128)(2,1)S(1)} %bitcast.19), channel_id=1, replica_groups=mesh['dp'=8,'space'=16] {'space'}, dimensions={0} | all-to-all | bytes 917504 | tf_op jit(solution)/shard_map/all_to_all | solution.py:364
  85.3 20.7 %conv_backward.1 = (bf16[96,7,16,448]{3,2,1,0:T(8,128)(2,1)}, f32[81,96]{1,0:T(8,128)}) custom-call(bf16[81,96]{1,0:T(8,128)(2,1)} %reshape.47.w_ref, bf16[512,448]{1,0:T(8,128)(2,1)} %bitcast.18, bf16[96,7,16,448]{3,2,1,0:T(8,128)(2,1)} %bitcast.14), custom_call_target="tpu_custom_call" | custom-call | tf_op jit(solution)/shard_map/conv_backward/pallas_call | solution.py:151
  105.9 0.8 broadcast_in_dim.25
  106.8 17.1 %all_to_all.26 = f32[16,81,96]{2,1,0:T(8,128)S(1)} all-to-all(f32[16,81,96]{2,1,0:T(8,128)S(1)} %broadcast_in_dim.25), channel_id=1, replica_groups=mesh['dp'=8,'space'=16] {'space'}, dimensions={0} | all-to-all | bytes 995328 | tf_op jit(solution)/shard_map/all_to_all | solution.py:349
  123.9 0.1 reduce_sum.27
  124.0 12.3 %all_to_all.27 = bf16[8,81,96]{2,1,0:T(8,128)(2,1)S(1)} all-to-all(bf16[8,81,96]{2,1,0:T(8,128)(2,1)S(1)} %broadcast_in_dim.26), channel_id=1, replica_groups=mesh['dp'=8,'space'=16] {'dp'}, dimensions={0} | all-to-all | bytes 248832 | tf_op jit(solution)/shard_map/all_to_all | solution.py:349
  136.3 11.5 %reduce-scatter.2.cloned.1.call-done = bf16[864,128]{1,0:T(8,128)(2,1)} async-done(((bf16[13824,128]{1,0:T(8,128)(2,1)}), bf16[864,128]{1,0:T(8,128)(2,1)}) %reduce-scatter.2.cloned.1.call-update) | async-done | bytes 221200 | tf_op jit(solution)/shard_map/reduce_scatter | solution.py:343
  147.8 2.4 %broadcast_in_dim.27 = bf16[8,864,128]{2,1,0:T(8,128)(2,1)} broadcast(bf16[864,128]{1,0:T(8,128)(2,1)} %reduce-scatter.2.cloned.1.call-done), dimensions={1,2} | broadcast | bytes 1990656 | tf_op jit(solution)/shard_map/broadcast_in_dim | solution.py:348
  150.2 4.5 %all-to-all-start.4 = ((bf16[8,864,128]{2,1,0:T(8,128)(2,1)}), bf16[8,864,128]{2,1,0:T(8,128)(2,1)S(1)}, u32[]{:S(2)}, u32[]{:S(2)}) async-start(bf16[8,864,128]{2,1,0:T(8,128)(2,1)} %broadcast_in_dim.27), calls=%async_computation.5 | async-start | bytes 3538944 | tf_op jit(solution)/shard_map/all_to_all | solution.py:349
  154.7 0.1 convert_reduce_fusion.1
  154.8 0.6 reshape.52
  155.4 20.0 %all-to-all-done.4 = bf16[8,864,128]{2,1,0:T(8,128)(2,1)S(1)} async-done(((bf16[8,864,128]{2,1,0:T(8,128)(2,1)}), bf16[8,864,128]{2,1,0:T(8,128)(2,1)S(1)}, u32[]{:S(2)}, u32[]{:S(2)}) %all-to-all-start.4) | async-done | bytes 1769504 | tf_op jit(solution)/shard_map/all_to_all | solution.py:349
  175.4 0.2 convert_reduce_fusion
  175.7 0.6 reshape.55
  176.3 0.7 reshape.57
  177.0 0.7 reshape.54
  177.7 0.7 reshape.56
  (4 shorter events, 0.1 us)
Async XLA Ops:
  8.5 20.6 %copy-start.2 = (f32[384]{0:T(512)S(1)}, f32[384]{0:T(512)}, u32[]{:S(2)}) copy-start(f32[384]{0:T(512)} %param.16) | copy-start | bytes 4612
  8.5 21.2 %copy-start.3 = (f32[384]{0:T(512)S(1)}, f32[384]{0:T(512)}, u32[]{:S(2)}) copy-start(f32[384]{0:T(512)} %param.19) | copy-start | bytes 4612
  21.8 19.5 %all-to-all-start = ((bf16[16,32,448]{2,1,0:T(8,128)(2,1)}), bf16[16,32,448]{2,1,0:T(8,128)(2,1)S(1)}, u32[]{:S(2)}, u32[]{:S(2)}) async-start(bf16[16,32,448]{2,1,0:T(8,128)(2,1)} %bitcast.17), calls=%async_computation | async-start | bytes 1048576 | tf_op jit(solution)/shard_map/all_to_all | solution.py:359
  28.9 118.9 %reduce-scatter.2.cloned.1.call-start = ((), (), s32[]{:S(2)}) async-start(), calls=%async_computation.6 | async-start | bytes 3760128 | tf_op jit(solution)/shard_map/reduce_scatter | solution.py:343
  41.2 0.8 copy-start
  68.6 1.0 copy-start.1
  150.2 25.2 %all-to-all-start.4 = ((bf16[8,864,128]{2,1,0:T(8,128)(2,1)}), bf16[8,864,128]{2,1,0:T(8,128)(2,1)S(1)}, u32[]{:S(2)}, u32[]{:S(2)}) async-start(bf16[8,864,128]{2,1,0:T(8,128)(2,1)} %broadcast_in_dim.27), calls=%async_computation.5 | async-start | bytes 3538944 | tf_op jit(solution)/shard_map/all_to_all | solution.py:349
Sparse Core Ops, SparseCore 0:
  68.8 79.0 reduce-scatter.1

commit v2 on v1

--- a/solution.py
+++ b/solution.py
@@ -103,8 +103,23 @@
     )(w81, features)
 
 
-def conv_backward_kernel(w_ref, v_ref, x_ref, fg_ref, conv_ref, band_ref, pg_ref, rows_ref, g_ref):
+def conv_backward_kernel(
+    w_ref, v_ref, sums_ref, x_ref,
+    fg_ref, conv_ref, qkv_ref, proj_ref, fc1_ref, fc2_ref,
+    band_ref, pg_ref, rows_ref, g_ref,
+):
     step = pl.program_id(0)
+
+    @pl.when(step == 1)
+    def _():
+        qkv_ref[...] = sums_ref[0].astype(F32)
+        proj_ref[...] = sums_ref[1, :, :384].astype(F32)
+        fc1_ref[:, :768] = sums_ref[1, :, 384:].astype(F32)
+        fc1_ref[:, 768:] = sums_ref[2, :, :768].astype(F32)
+        fc2_ref[0:24] = sums_ref[2, :, 768:].astype(F32)
+        for quarter in range(3):
+            at = quarter * 24 + 24
+            fc2_ref[at : at + 24] = sums_ref[3, :, quarter * 384 : quarter * 384 + 384].astype(F32)
 
     @pl.when(step == 0)
     def _():
@@ -123,6 +138,7 @@
                     at = (row * 9 + e * 3 + o) * 16
                     pg_ref[at : at + 16, :] = moved.astype(BF)
         g_ref[...] = jnp.zeros_like(g_ref)
+        conv_ref[...] = jnp.zeros_like(conv_ref)
 
     x = x_ref[:, 0].reshape(1536, 448)
     pg = pg_ref[pl.ds(pl.multiple_of(step * 144, 16), 432), :448]
@@ -144,25 +160,35 @@
             high = total.astype(BF)
             rest = total - high.astype(F32)
             middle = rest.astype(BF)
-            conv_ref[a * 27 : (a + 1) * 27, :] = dot(high, spread) + dot(middle, spread)
-
-
-def conv_backward(features, w81, grad_rows):
+            conv_ref[a * 27 : (a + 1) * 27, :96] = dot(high, spread) + dot(middle, spread)
+
+
+def conv_backward(features, w81, grad_rows, sums):
+    whole = lambda *shape: pl.BlockSpec(shape, lambda h: (0,) * len(shape))
     return pl.pallas_call(
         conv_backward_kernel,
         grid=(7,),
         out_shape=(
             jax.ShapeDtypeStruct((96, 7, 16, 448), BF),
-            jax.ShapeDtypeStruct((81, 96), F32),
+            jax.ShapeDtypeStruct((128, 128), F32),
+            jax.ShapeDtypeStruct((24, 1152), F32),
+            jax.ShapeDtypeStruct((24, 384), F32),
+            jax.ShapeDtypeStruct((24, 1536), F32),
+            jax.ShapeDtypeStruct((96, 384), F32),
         ),
         in_specs=[
-            pl.BlockSpec((81, 96), lambda h: (0, 0)),
-            pl.BlockSpec((512, 448), lambda h: (0, 0)),
+            whole(81, 96),
+            whole(512, 448),
+            whole(4, 24, 1152),
             pl.BlockSpec((96, 1, 16, 448), lambda h: (0, h, 0, 0)),
         ],
         out_specs=(
             pl.BlockSpec((96, 1, 16, 448), lambda h: (0, h, 0, 0)),
-            pl.BlockSpec((81, 96), lambda h: (0, 0)),
+            whole(128, 128),
+            whole(24, 1152),
+            whole(24, 384),
+            whole(24, 1536),
+            whole(96, 384),
         ),
         scratch_shapes=[
             pltpu.VMEM((1536, 432), BF),
@@ -171,7 +197,7 @@
             pltpu.VMEM((432, 1536), F32),
         ],
         name="conv_backward",
-    )(w81, grad_rows, features)
+    )(w81, grad_rows, sums, features)
 
 
 def patch_matrix(patch_weight):
@@ -203,8 +229,8 @@
 
 def frame_kernel(
     z_ref, g_ref, pos_ref, pw_ref, n1_ref, wqkv_ref, wproj_ref, n2_ref, w1_ref, w2_ref,
-    out_ref, dz_ref, dqkv_ref, dproj_ref, d1_ref, d2_ref,
-    wp_ref, a_ref, r_ref, pk_ref, dpk_ref, prob_ref,
+    out_ref, dz_ref, dw_ref,
+    wp_ref, a_ref, r_ref, pk_ref, dpk_ref, prob_ref, d2_ref,
 ):
     wp_ref[...] = patch_matrix(pw_ref[...])
     z = z_ref[...].astype(F32)
@@ -252,23 +278,30 @@
     g = g_ref[...]
     out = residual
     dnormed2 = jnp.zeros((256, 384), F32)
-    for part in range(3):
-        cols = slice(part * 512, part * 512 + 512)
+    for part in range(2):
+        cols = slice(part * 768, part * 768 + 768)
         pre = dot(normed2, w1_ref[:, cols])
         cdf = 0.5 + 0.5 * lax.erf(pre * 0.7071067811865476)
         hidden = (pre * cdf).astype(BF)
         out = out + dot(hidden, w2_ref[cols, :])
-        d2_ref[cols, :] = dot(hidden, g, TN).astype(BF)
+        d2 = dot(hidden, g, TN)
+        for piece in range(32):
+            tile_at, quarter = part * 8 + piece // 4, piece % 4
+            d2_ref[quarter, tile_at * 24 : tile_at * 24 + 24, :] = d2[piece * 24 : piece * 24 + 24]
         dhidden = dot(g, w2_ref[cols, :], NT).astype(BF).astype(F32)
         slope = cdf + pre * (0.3989422804014327 * jnp.exp(-0.5 * pre * pre))
         dpre = (dhidden * slope).astype(BF)
-        d1_ref[:, cols] = dot(normed2, dpre, TN).astype(BF)
+        d1 = dot(normed2, dpre, TN).astype(BF)
+        dw_ref[1 + part, :, 384 * (1 - part) : 384 * (1 - part) + 768] = d1
         dnormed2 = dnormed2 + dot(dpre, w1_ref[:, cols], NT)
     out_ref[...] = out.astype(BF)
+    dw_ref[2, :, 768:] = d2_ref[0].astype(BF)
+    for quarter in range(3):
+        dw_ref[3, :, quarter * 384 : quarter * 384 + 384] = d2_ref[1 + quarter].astype(BF)
     dnormed2 = dnormed2.astype(BF).astype(F32)
     dres = g.astype(F32) + norm_backward(unit2, scale2, gain2, dnormed2)
     dres_bf = dres.astype(BF)
-    dproj_ref[...] = dot(attended, dres_bf, TN).astype(BF)
+    dw_ref[1, :, :384] = dot(attended, dres_bf, TN).astype(BF)
     datt = dot(dres_bf, wproj_ref[...], NT).astype(BF)
     for pair in range(3):
         q = pk_ref[:, pair * 128 : pair * 128 + 128]
@@ -289,7 +322,7 @@
         dpk_ref[:, 384 + pair * 128 : 384 + pair * 128 + 128] = jnp.where(left, dk[0], dk[1]).astype(BF)
         dpk_ref[:, 768 + pair * 128 : 768 + pair * 128 + 128] = jnp.where(left, dv[0], dv[1]).astype(BF)
     dpk = dpk_ref[...]
-    dqkv_ref[...] = dot(normed, dpk, TN).astype(BF)
+    dw_ref[0] = dot(normed, dpk, TN).astype(BF)
     dnormed = dot(dpk, wqkv_ref[...], NT).astype(BF).astype(F32)
     demb = dres + norm_backward(unit1, scale1, gain1, dnormed)
     a_ref[...] = dot(demb.astype(BF), wp_ref[...], NT)
@@ -315,10 +348,7 @@
         out_shape=(
             jax.ShapeDtypeStruct((256, 384), BF),
             jax.ShapeDtypeStruct((512, 448), BF),
-            jax.ShapeDtypeStruct((384, 1152), BF),
-            jax.ShapeDtypeStruct((384, 384), BF),
-            jax.ShapeDtypeStruct((384, 1536), BF),
-            jax.ShapeDtypeStruct((1536, 384), BF),
+            jax.ShapeDtypeStruct((4, 384, 1152), BF),
         ),
         scratch_shapes=[
             pltpu.VMEM((896, 384), BF),
@@ -327,26 +357,254 @@
             pltpu.VMEM((256, 1152), BF),
             pltpu.VMEM((256, 1152), BF),
             pltpu.VMEM((6, 256, 256), F32),
+            pltpu.VMEM((4, 384, 384), F32),
         ],
         name="frame_step",
     )(z, g, pos, pw, n1, wqkv, wproj, n2, w1, w2)
 
 
-def in_blocks(x, length):
-    return x.reshape(length, x.shape[0] // length, *x.shape[1:])
-
-
-def one_scatter(arrays, axis):
-    length = lax.axis_size(axis)
-    blocks = [in_blocks(a, length) for a in arrays]
-    lines = jnp.concatenate([b.reshape(length, -1, 128) for b in blocks], axis=1).reshape(-1, 128)
-    mine = lax.psum_scatter(lines, axis, tiled=True)
-    return mine, blocks
-
-
-def from_everyone(x, axis):
-    copies = jnp.broadcast_to(x, (lax.axis_size(axis), *x.shape))
-    return lax.all_to_all(copies, axis, split_axis=0, concat_axis=0, tiled=True)
+def flip(i):
+    return i + 1 - 2 * (i % 2)
+
+
+def across(i):
+    return (i + 2) % 4
+
+
+def mirror(i):
+    return 3 - i
+
+
+class Mailer:
+    def __init__(self, send, recv):
+        self.send, self.recv, self.count, self.copies = send, recv, 0, []
+
+    def __call__(self, source, target, **where):
+        copy = pltpu.make_async_remote_copy(
+            src_ref=source,
+            dst_ref=target,
+            send_sem=self.send.at[self.count],
+            recv_sem=self.recv.at[self.count],
+            device_id=where,
+            device_id_type=pl.DeviceIdType.MESH,
+        )
+        self.count += 1
+        copy.start()
+        self.copies.append(copy)
+        return copy
+
+
+def meet(peers):
+    barrier = pltpu.get_barrier_semaphore()
+    for where in peers:
+        pl.semaphore_signal(barrier, inc=1, device_id=where, device_id_type=pl.DeviceIdType.MESH)
+    pl.semaphore_wait(barrier, len(peers))
+
+
+def exchange_kernel(x_ref, o_ref, send, recv, local):
+    me = lax.axis_index("space")
+    peers = [(me + k) % 16 for k in range(1, 16)]
+    own = pltpu.make_async_copy(x_ref.at[me], o_ref.at[me], local)
+    own.start()
+    meet([{"space": peer} for peer in peers])
+    mail = Mailer(send, recv)
+    copies = [mail(x_ref.at[peer], o_ref.at[me], space=peer) for peer in peers]
+    own.wait()
+    for copy in copies:
+        copy.wait()
+
+
+def exchange(rows):
+    return pl.pallas_call(
+        exchange_kernel,
+        out_shape=jax.ShapeDtypeStruct(rows.shape, rows.dtype),
+        in_specs=[pl.BlockSpec(memory_space=pl.ANY)],
+        out_specs=pl.BlockSpec(memory_space=pl.ANY),
+        scratch_shapes=[
+            pltpu.SemaphoreType.DMA((15,)),
+            pltpu.SemaphoreType.DMA((15,)),
+            pltpu.SemaphoreType.DMA,
+        ],
+        compiler_params=pltpu.CompilerParams(collective_id=0, has_side_effects=True),
+        name="exchange",
+    )(rows)
+
+
+def accumulate(target, first, sources):
+    count = sources[0].shape[0]
+
+    def body(i, carry):
+        total = target[first + i].astype(F32)
+        for source in sources:
+            total = total + source[i].astype(F32)
+        target[first + i] = total.astype(BF)
+        return carry
+
+    lax.fori_loop(0, count, body, 0)
+
+
+def reduce_kernel(
+    rows_ref, w_ref, rows_out, sums_ref,
+    own, got, z1, z2, y1, y2, x_in, mine, send, recv, local,
+):
+    space, dp = lax.axis_index("space"), lax.axis_index("dp")
+    y, x_hi, core = space // 4, space // 2 % 2, space % 2
+    x_lo, z = dp // 4, dp % 4
+    peers = [(space + k) % 16 for k in range(1, 16)]
+
+    def at(y_to=y, x_hi_to=x_hi, x_lo_to=x_lo, z_to=z, core_to=core):
+        return {"dp": x_lo_to * 4 + z_to, "space": y_to * 4 + x_hi_to * 2 + core_to}
+
+    quarters = [across(z), flip(z), mirror(z), z]
+    loads = [pltpu.make_async_copy(w_ref.at[q, :, core], own.at[i], local.at[i]) for i, q in enumerate(quarters)]
+    for load in loads:
+        load.start()
+    own_rows = pltpu.make_async_copy(rows_ref.at[space], rows_out.at[space], local.at[4])
+    own_rows.start()
+    meet(
+        [{"dp": dp, "space": peer} for peer in peers]
+        + [at(z_to=flip(z)), at(z_to=mirror(z)), at(z_to=across(z))]
+        + [at(x_lo_to=1 - x_lo), at(x_hi_to=1 - x_hi, x_lo_to=1 - x_lo)]
+    )
+    mail = Mailer(send, recv)
+    rows = [mail(rows_ref.at[peer], rows_out.at[space], dp=dp, space=peer) for peer in peers]
+    pair = [mail(w_ref.at[q, :, 1 - core], got.at[i], **at(core_to=1 - core)) for i, q in enumerate(quarters)]
+    first = []
+    for i in range(4):
+        loads[i].wait()
+        pair[i].wait_recv()
+        accumulate(own.at[i], 0, [got.at[i]])
+        if i < 2:
+            first.append(mail(own.at[i, 0:4], z1.at[i], **at(z_to=flip(z))))
+        if i % 2 == 0:
+            first.append(mail(own.at[i, 4:8], z1.at[2 + i // 2], **at(z_to=mirror(z))))
+    low0, high0, low1, high1 = first
+    low0.wait_recv()
+    accumulate(own.at[2], 0, [z1.at[0]])
+    low2 = mail(own.at[2, 0:4], z2.at[0], **at(z_to=mirror(z)))
+    high0.wait_recv()
+    accumulate(own.at[1], 4, [z1.at[2]])
+    high2 = mail(own.at[1, 4:8], z2.at[1], **at(z_to=flip(z)))
+    low1.wait_recv()
+    low2.wait_recv()
+    accumulate(own.at[3], 0, [z1.at[1], z2.at[0]])
+    high1.wait_recv()
+    high2.wait_recv()
+    accumulate(own.at[3], 4, [z1.at[3], z2.at[1]])
+    block = lambda y_of, x_of: own.at[3, pl.ds(y_of * 2 + x_of, 1)]
+    low0 = mail(block(across(y), 0), y1.at[0], **at(y_to=flip(y)))
+    high0 = mail(block(across(y), 1), y1.at[2], **at(y_to=mirror(y)))
+    low1 = mail(block(flip(y), 0), y1.at[1], **at(y_to=flip(y)))
+    high1 = mail(block(mirror(y), 1), y1.at[3], **at(y_to=mirror(y)))
+    low0.wait_recv()
+    accumulate(own.at[3], mirror(y) * 2, [y1.at[0]])
+    low2 = mail(block(mirror(y), 0), y2.at[0], **at(y_to=mirror(y)))
+    high0.wait_recv()
+    accumulate(own.at[3], flip(y) * 2 + 1, [y1.at[2]])
+    high2 = mail(block(flip(y), 1), y2.at[1], **at(y_to=flip(y)))
+    low1.wait_recv()
+    low2.wait_recv()
+    accumulate(own.at[3], y * 2, [y1.at[1], y2.at[0]])
+    high1.wait_recv()
+    high2.wait_recv()
+    accumulate(own.at[3], y * 2 + 1, [y1.at[3], y2.at[1]])
+    x_mine = x_hi * 2 + x_lo
+    lines = [
+        mail(own.at[3, y * 2 + hi], x_in.at[x_mine], **at(x_hi_to=hi, x_lo_to=lo))
+        for hi, lo in ((1 - x_hi, x_lo), (x_hi, 1 - x_lo), (1 - x_hi, 1 - x_lo))
+    ]
+    x_in[x_mine] = own[3, y * 2 + x_hi]
+    for line in lines:
+        line.wait_recv()
+    total = x_in[0].astype(F32)
+    for i in range(1, 4):
+        total = total + x_in[i].astype(F32)
+    mine[...] = total.astype(BF)
+    sums_ref[z] = total.astype(BF)
+    spread = [mail(mine, sums_ref.at[z], **at(z_to=to)) for to in (flip(z), mirror(z), across(z))]
+    own_rows.wait()
+    for copy in rows + spread:
+        copy.wait_recv()
+    for copy in mail.copies:
+        copy.wait_send()
+
+
+def reduce_all(rows, weights):
+    piece = (24, 1152)
+    copies = 37
+    return pl.pallas_call(
+        reduce_kernel,
+        out_shape=(
+            jax.ShapeDtypeStruct(rows.shape, BF),
+            jax.ShapeDtypeStruct((4, *piece), BF),
+        ),
+        in_specs=[pl.BlockSpec(memory_space=pl.ANY)] * 2,
+        out_specs=(pl.BlockSpec(memory_space=pl.ANY), pl.BlockSpec(memory_space=pltpu.VMEM)),
+        scratch_shapes=[
+            pltpu.VMEM((4, 8, *piece), BF),
+            pltpu.VMEM((4, 8, *piece), BF),
+            pltpu.VMEM((4, 4, *piece), BF),
+            pltpu.VMEM((2, 4, *piece), BF),
+            pltpu.VMEM((4, 1, *piece), BF),
+            pltpu.VMEM((2, 1, *piece), BF),
+            pltpu.VMEM((4, *piece), BF),
+            pltpu.VMEM(piece, BF),
+            pltpu.SemaphoreType.DMA((copies,)),
+            pltpu.SemaphoreType.DMA((copies,)),
+            pltpu.SemaphoreType.DMA((5,)),
+        ],
+        compiler_params=pltpu.CompilerParams(collective_id=1, has_side_effects=True),
+        name="reduce_all",
+    )(rows, weights.reshape(4, 8, 2, 24, 1152))
+
+
+def conv_total_kernel(part_ref, total_ref, by_space, by_dp, send, recv):
+    space, dp = lax.axis_index("space"), lax.axis_index("dp")
+    across_space = [(space + k) % 16 for k in range(1, 16)]
+    across_dp = [(dp + k) % 8 for k in range(1, 8)]
+    meet(
+        [{"dp": dp, "space": peer} for peer in across_space]
+        + [{"dp": peer, "space": space} for peer in across_dp]
+    )
+    mail = Mailer(send, recv)
+    lines = lambda i: pl.ds(pl.multiple_of(i * 8, 8), 8)
+    one = [mail(part_ref.at[lines(to)], by_space.at[space], dp=dp, space=to) for to in across_space]
+    by_space[space] = part_ref[lines(space), :]
+    for copy in one:
+        copy.wait_recv()
+    total = by_space[0]
+    for i in range(1, 16):
+        total = total + by_space[i]
+    by_dp[dp] = total
+    two = [mail(by_dp.at[dp], by_dp.at[dp], dp=to, space=space) for to in across_dp]
+    for copy in two:
+        copy.wait_recv()
+    total = by_dp[0]
+    for i in range(1, 8):
+        total = total + by_dp[i]
+    total_ref[lines(space), :] = total
+    three = [mail(total_ref.at[lines(space)], total_ref.at[lines(space)], dp=dp, space=to) for to in across_space]
+    for copy in three:
+        copy.wait_recv()
+    for copy in mail.copies:
+        copy.wait_send()
+
+
+def conv_total(part):
+    return pl.pallas_call(
+        conv_total_kernel,
+        out_shape=jax.ShapeDtypeStruct((128, 128), F32),
+        in_specs=[pl.BlockSpec(memory_space=pltpu.VMEM)],
+        out_specs=pl.BlockSpec(memory_space=pltpu.VMEM),
+        scratch_shapes=[
+            pltpu.VMEM((16, 8, 128), F32),
+            pltpu.VMEM((8, 8, 128), F32),
+            pltpu.SemaphoreType.DMA((37,)),
+            pltpu.SemaphoreType.DMA((37,)),
+        ],
+        compiler_params=pltpu.CompilerParams(collective_id=2, has_side_effects=True),
+        name="conv_total",
+    )(part)
 
 
 def shards(
@@ -355,30 +613,18 @@
 ):
     tile = features[0].transpose(0, 2, 1, 3)
     w81 = conv_weight.reshape(81, 96)
-    rows = conv_forward(tile, w81).reshape(16, 32, 448)
-    rows = lax.all_to_all(rows, "space", split_axis=0, concat_axis=0, tiled=True)
-    block_out, grad_rows, dqkv, dproj, d1, d2 = frame_step(
+    rows = exchange(conv_forward(tile, w81).reshape(16, 32, 448))
+    block_out, grad_rows, weights = frame_step(
         rows.reshape(512, 448), out_grad[0, 0], pos_embed, patch_weight, norm1[None],
         qkv_weight, proj_weight, norm2[None], fc1_weight, fc2_weight,
     )
-    grad_rows = lax.all_to_all(
-        grad_rows.reshape(16, 32, 448), "space", split_axis=0, concat_axis=0, tiled=True
-    )
-    feature_grad, conv_part = conv_backward(tile, w81, grad_rows.reshape(512, 448))
-    mine, blocks = one_scatter((dqkv, dproj, d1, d2), "space")
-    conv_space = from_everyone(conv_part, "space").sum(axis=0)
-    total = from_everyone(mine, "dp").astype(F32).sum(axis=0)
-    conv_total = from_everyone(conv_space.astype(BF), "dp").astype(F32).sum(axis=0)
-    shares, at = [], 0
-    for b in blocks:
-        part = b[0]
-        lines = part.size // 128
-        shares.append(total[at : at + lines].reshape(part.shape))
-        at += lines
+    grad_rows, sums = reduce_all(grad_rows.reshape(16, 32, 448), weights)
+    feature_grad, conv_part, *shares = conv_backward(tile, w81, grad_rows.reshape(512, 448), sums)
+    conv_sum = conv_total(conv_part)
     return (
         block_out[None, None],
         feature_grad.transpose(0, 2, 1, 3)[None],
-        conv_total.reshape(conv_weight.shape),
+        conv_sum[:81, :96].reshape(conv_weight.shape),
         *shares,
     )
 

time: 186 us -> 135 us (0.73)
  Pallas kernels: 50.1 us -> 127 us
  blocking collectives: 45 us -> 0 us
  waiting for transfers between devices: 42.5 us -> 0 us
  local copies, waits for them, and re-layouts: 19.3 us -> 5.3 us
  between operations: 14.1 us -> 0.66 us
  starting transfers between devices: 11.8 us -> 0 us
  other arithmetic: 2.3 us -> 0 us
    pallas_call x0 -> x3, Pallas kernels: none -> 76.6 us  [the longest x1 42 us: reduce_all(): pl.pallas_call(reduce_kernel, out_shape=(jax.ShapeDtypeStruct(rows.shape,...]
    all_to_all x3 -> x0, blocking collectives: 45 us -> none  [the longest x2 29.4 us: from_everyone(): return lax.all_to_all(copies, axis, split_axis=0, concat_axis=0, tiled=True)]
    all_to_all x2 -> x0, waiting for transfers between devices: 30.9 us -> none  [the longest x1 20 us: from_everyone(): return lax.all_to_all(copies, axis, split_axis=0, concat_axis=0, tiled=True)]
    all_to_all x2 -> x0, starting transfers between devices: 11.6 us -> none  [the longest x1 7.14 us: shards(): lax.all_to_all(rows, 'space', split_axis=0, concat_axis=0, tiled=True)]
    reduce_scatter x1 -> x0, waiting for transfers between devices: 11.5 us -> none  [one_scatter(): mine = lax.psum_scatter(lines, axis, tiled=True)]
    another operation x4 -> x0, local copies, waits for them, and re-layouts: 8.42 us -> none  [one_scatter(): b.reshape(length, -1, 128)]
    broadcast_in_dim x3 -> x0, local copies, waits for them, and re-layouts: 3.25 us -> none  [from_everyone(): copies = jnp.broadcast_to(x, (lax.axis_size(axis), *x.shape))]
    reshape x5 -> x1, local copies, waits for them, and re-layouts: 3.31 us -> 0.64 us  [shards(): conv_sum[:81, :96].reshape(conv_weight.shape)]
  transfers between devices with their start and end apart: 3 -> 0, of which waited for: 3 -> 0; matrix products, arithmetic and copies ran while one was open for 2% -> 0% of each run, Pallas kernels for 11% -> 0%
where the time goes in v2:
time: 135 us; the launch traced here: 133 us
  Pallas kernels  127 us (94%)
  local copies, waits for them, and re-layouts  5.3 us (4%)
    pallas_call x1, Pallas kernels, reduce_all(): pl.pallas_call(reduce_kernel, out_shape=(jax.ShapeDtypeStruct(rows.shape,...  42 us
    pallas_call x1, Pallas kernels, conv_total(): pl.pallas_call(conv_total_kernel, out_shape=jax.ShapeDtypeStruct((128, 12...  21 us
    pallas_call x1, Pallas kernels, conv_backward(): pl.pallas_call(conv_backward_kernel, grid=(7,), out_shape=(jax.ShapeDtype...  20.8 us
    pallas_call x1, Pallas kernels, frame_step(): pl.pallas_call(frame_kernel, out_shape=(jax.ShapeDtypeStruct((256, 384),...  16.6 us
    pallas_call x1, Pallas kernels, exchange(): pl.pallas_call(exchange_kernel, out_shape=jax.ShapeDtypeStruct(rows.shape...  13.7 us
    pallas_call x1, Pallas kernels, conv_forward(): pl.pallas_call(conv_forward_kernel, grid=(7,), out_shape=jax.ShapeDtypeSt...  13.2 us

profile of v2, /device:TPU:0, one launch (start us, length us, event | category | flops | bytes accessed | tf_op | source)
XLA Modules:
  0.0 133.2 jit_solution(13236033918911134593)
XLA Ops:
  0.6 1.2 broadcast_in_dim.12.n1_ref
  1.9 1.2 broadcast_in_dim.13.n2_ref
  3.1 1.4 %reshape.35.w_ref = bf16[81,96]{1,0:T(8,128)(2,1)} reshape(bf16[3,3,3,3,96]{4,3,2,1,0:T(4,128)(2,1)} %param.12) | data formatting | bytes 31104 | tf_op jit(solution)/shard_map/reshape | solution.py:615
  4.5 13.2 %conv_forward.1 = bf16[512,448]{1,0:T(8,128)(2,1)} custom-call(bf16[81,96]{1,0:T(8,128)(2,1)} %reshape.35.w_ref, bf16[96,7,16,448]{3,2,1,0:T(8,128)(2,1)} %bitcast.13), custom_call_target="tpu_custom_call" | custom-call | tf_op jit(solution)/shard_map/conv_forward/pallas_call | solution.py:88
  17.7 13.7 %exchange.1 = bf16[16,32,448]{2,1,0:T(8,128)(2,1)} custom-call(bf16[16,32,448]{2,1,0:T(8,128)(2,1)} %bitcast.17), custom_call_target="tpu_custom_call" | custom-call | tf_op jit(solution)/shard_map/exchange/pallas_call | solution.py:418
  31.3 16.6 %frame_step.1 = (bf16[256,384]{1,0:T(8,128)(2,1)}, bf16[512,448]{1,0:T(8,128)(2,1)}, bf16[4,384,1152]{2,1,0:T(8,128)(2,1)}) custom-call(bf16[512,448]{1,0:T(8,128)(2,1)} %bitcast.16, bf16[256,384]{1,0:T(8,128)(2,1)} %bitcast.20, bf16[256,384]{1,0:T(8,128)(2,1)} %pos_ref.1, bf16[588,384]{1,0:T(8,128)(2,1)} %pw_ref.1, f32[1,384]{1,0:T(1,128)} %broadcast_in_dim.12.n1_ref, ...), custom_call_target="tpu_custom_call" | custom-call | tf_op jit(solution)/shard_map/frame_step/pallas_call | solution.py:346
  48.0 42.0 %reduce_all.1 = (bf16[16,32,448]{2,1,0:T(8,128)(2,1)}, bf16[4,24,1152]{2,1,0:T(8,128)(2,1)}) custom-call(bf16[16,32,448]{2,1,0:T(8,128)(2,1)} %bitcast.18, bf16[4,8,2,24,1152]{4,3,2,1,0:T(8,128)(2,1)} %bitcast.15), custom_call_target="tpu_custom_call" | custom-call | tf_op jit(solution)/shard_map/reduce_all/pallas_call | solution.py:535
  90.0 20.8 %conv_backward.1 = (bf16[96,7,16,448]{3,2,1,0:T(8,128)(2,1)}, f32[128,128]{1,0:T(8,128)}, f32[24,1152]{1,0:T(8,128)}, f32[24,384]{1,0:T(8,128)}, f32[24,1536]{1,0:T(8,128)}, /*index=5*/f32[96,384]{1,0:T(8,128)}) custom-call(bf16[81,96]{1,0:T(8,128)(2,1)} %reshape.35.w_ref, bf16[512,448]{1,0:T(8,128)(2,1)} %bitcast.19, ...), custom_call_target="tpu_custom_call" | custom-call | tf_op jit(solution)/shard_map/conv_backward/pallas_call | solution.py:168
  110.7 21.0 %conv_total.1 = f32[128,128]{1,0:T(8,128)} custom-call(f32[128,128]{1,0:T(8,128)} %get-tuple-element.24.part_ref), custom_call_target="tpu_custom_call" | custom-call | tf_op jit(solution)/shard_map/conv_total/pallas_call | solution.py:594
  131.7 0.8 slice.3
  132.5 0.6 reshape.41

commit v3 on v2

v3 whole, which is shorter than its diff:
```python
import functools

import jax
import jax.numpy as jnp
from jax import lax
from jax.experimental import pallas as pl
from jax.experimental.pallas import tpu as pltpu
from jax.sharding import PartitionSpec as P

HEADS = 6
BF = jnp.bfloat16
F32 = jnp.float32
NN = (((1,), (0,)), ((), ()))
NT = (((1,), (1,)), ((), ()))
TN = (((0,), (0,)), ((), ()))


def dot(a, b, dims=NN):
    return lax.dot_general(a, b, dims, preferred_element_type=F32)


def iota(shape, dim):
    return lax.broadcasted_iota(jnp.int32, shape, dim)


def one_hot(cond):
    return jnp.where(cond, 1.0, 0.0).astype(BF)


def tap_rows(w, a):
    rows = [
        jnp.broadcast_to(w[a, 2 - b, e, o : o + 1, :], (16, 96))
        for b in range(3)
        for e in range(3)
        for o in range(3)
    ]
    return jnp.concatenate(rows, axis=0).astype(BF)


def band(w):
    spread = one_hot(iota((96, 1536), 1) // 16 == iota((96, 1536), 0))
    lag = iota((432, 1536), 1) % 16 - iota((432, 1536), 0) % 16 + 2
    total = None
    for a in range(3):
        piece = jnp.where(lag == a, dot(tap_rows(w, a), spread), 0.0)
        total = piece if total is None else total + piece
    return total.astype(BF)


def band_transposed(w):
    spread = one_hot(iota((1536, 96), 0) // 16 == iota((1536, 96), 1))
    lag = iota((1536, 432), 0) % 16 - iota((1536, 432), 1) % 16 + 2
    total = None
    for a in range(3):
        piece = jnp.where(lag == a, dot(spread, tap_rows(w, a), NT), 0.0)
        total = piece if total is None else total + piece
    return total.astype(BF)


def batch_place(row, colour):
    return (row // 5, (row % 5) * 3 + colour)


def conv_forward_kernel(w_ref, x_ref, out_ref, band_ref, acc_ref, rows_ref, post, send, recv, local):
    step = pl.program_id(0)
    me = lax.axis_index("space")
    peers = [(me + k) % 16 for k in range(1, 16)]

    @pl.when(step == 0)
    def _():
        barrier = pltpu.get_barrier_semaphore()
        for peer in peers:
            pl.semaphore_signal(
                barrier, inc=1, device_id={"space": peer}, device_id_type=pl.DeviceIdType.MESH
            )
        band_ref[...] = band(w_ref[...].astype(F32))
        acc_ref[...] = jnp.zeros_like(acc_ref)
        rows_ref[...] = jnp.zeros_like(rows_ref)

    x = x_ref[:, 0].reshape(1536, 448)
    at = pl.ds(pl.multiple_of(step * 144, 16), 432)
    acc_ref[at, :448] += dot(band_ref[...], x)

    def copies(batch):
        return [
            pltpu.make_async_remote_copy(
                src_ref=post.at[batch, peer],
                dst_ref=out_ref.at[batch, me],
                send_sem=send.at[batch * 15 + i],
                recv_sem=recv.at[batch * 15 + i],
                device_id={"space": peer},
                device_id_type=pl.DeviceIdType.MESH,
            )
            for i, peer in enumerate(peers)
        ]

    def mail(batch):
        for row in range(5) if batch == 0 else range(5, 9):
            taps = acc_ref[row * 144 : (row + 1) * 144, :]
            out = pltpu.roll(taps[0:48], 1, 1) + taps[48:96] + pltpu.roll(taps[96:144], 511, 1)
            for o in range(3):
                for t in range(4):
                    rows_ref[t, pl.ds(batch_place(row, o)[1], 16, stride=16), :] = out[
                        o * 16 : (o + 1) * 16, t * 128 : t * 128 + 128
                    ]
        for t in range(3):
            post[batch, :, :, t * 128 : t * 128 + 128] = rows_ref[t].reshape(16, 16, 128).astype(BF)
        post[batch, :, :, 384:448] = rows_ref[3, :, :64].reshape(16, 16, 64).astype(BF)
        for copy in copies(batch):
            copy.start()
        pltpu.make_async_copy(post.at[batch, me], out_ref.at[batch, me], local.at[batch]).start()

    @pl.when(step == 4)
    def _():
        pl.semaphore_wait(pltpu.get_barrier_semaphore(), 15)
        mail(0)

    @pl.when(step == 6)
    def _():
        mail(1)
        for batch in range(2):
            pltpu.make_async_copy(post.at[batch, me], out_ref.at[batch, me], local.at[batch]).wait()
            for copy in copies(batch):
                copy.wait()


def conv_forward(features, conv_weight):
    return pl.pallas_call(
        conv_forward_kernel,
        grid=(7,),
        out_shape=jax.ShapeDtypeStruct((2, 16, 16, 448), BF),
        in_specs=[
            pl.BlockSpec((3, 3, 3, 3, 96), lambda h: (0, 0, 0, 0, 0)),
            pl.BlockSpec((96, 1, 16, 448), lambda h: (0, h, 0, 0)),
        ],
        out_specs=pl.BlockSpec(memory_space=pl.ANY),
        scratch_shapes=[
            pltpu.VMEM((432, 1536), BF),
            pltpu.VMEM((1296, 512), F32),
            pltpu.VMEM((4, 256, 128), F32),
            pltpu.VMEM((2, 16, 16, 448), BF),
            pltpu.SemaphoreType.DMA((30,)),
            pltpu.SemaphoreType.DMA((30,)),
            pltpu.SemaphoreType.DMA((2,)),
        ],
        compiler_params=pltpu.CompilerParams(collective_id=0, has_side_effects=True),
        name="conv_forward",
    )(conv_weight, features)


def feature_gradient_kernel(band_ref, pg_ref, sums_ref, fg_ref, qkv_ref, proj_ref, fc1_ref, fc2_ref):
    step = pl.program_id(0)

    @pl.when(step == 1)
    def _():
        qkv_ref[...] = sums_ref[0].astype(F32)
        proj_ref[...] = sums_ref[1, :, :384].astype(F32)
        fc1_ref[:, :768] = sums_ref[1, :, 384:].astype(F32)
        fc1_ref[:, 768:] = sums_ref[2, :, :768].astype(F32)
        fc2_ref[0:24] = sums_ref[2, :, 768:].astype(F32)
        for quarter in range(3):
            at = quarter * 24 + 24
            fc2_ref[at : at + 24] = sums_ref[3, :, quarter * 384 : quarter * 384 + 384].astype(F32)

    pg = pg_ref[pl.ds(pl.multiple_of(step * 144, 16), 432), :448]
    fg_ref[:, 0] = dot(band_ref[...], pg).astype(BF).reshape(96, 16, 448)


def feature_gradient(back, pixel_taps, sums):
    whole = lambda *shape: pl.BlockSpec(shape, lambda h: (0,) * len(shape))
    return pl.pallas_call(
        feature_gradient_kernel,
        grid=(7,),
        out_shape=(
            jax.ShapeDtypeStruct((96, 7, 16, 448), BF),
            jax.ShapeDtypeStruct((24, 1152), F32),
            jax.ShapeDtypeStruct((24, 384), F32),
            jax.ShapeDtypeStruct((24, 1536), F32),
            jax.ShapeDtypeStruct((96, 384), F32),
        ),
        in_specs=[whole(1536, 432), whole(1296, 512), whole(4, 24, 1152)],
        out_specs=(
            pl.BlockSpec((96, 1, 16, 448), lambda h: (0, h, 0, 0)),
            whole(24, 1152),
            whole(24, 384),
            whole(24, 1536),
            whole(96, 384),
        ),
        name="feature_gradient",
    )(back, pixel_taps, sums)


def patch_matrix(patch_weight):
    row = iota((896, 588), 0)
    tile_row = row % 32
    place = tile_row - tile_row // 16
    colour, height = place % 3, place // 3
    piece = row // 32
    half, column = piece // 14, piece % 14
    line = (7 * half + height + 13) % 14
    source = colour * 196 + line * 14 + column
    return dot(one_hot((iota((896, 588), 1) == source) & (tile_row < 28) & (tile_row != 15)), patch_weight).astype(BF)


def norm_forward(values, gain):
    centered = values - jnp.mean(values, axis=-1, keepdims=True)
    scale = lax.rsqrt(jnp.mean(centered * centered, axis=-1, keepdims=True) + 1e-06)
    unit = centered * scale
    return unit, scale, (unit * gain).astype(BF)


def norm_backward(unit, scale, gain, grad):
    grad = grad * gain
    return scale * (
        grad
        - jnp.mean(grad, axis=-1, keepdims=True)
        - unit * jnp.mean(grad * unit, axis=-1, keepdims=True)
    )


def frame_kernel(
    z_ref, g_ref, pos_ref, pw_ref, n1_ref, wqkv_ref, wproj_ref, n2_ref, w1_ref, w2_ref,
    out_ref, dz_ref, dw_ref,
    wp_ref, a_ref, r_ref, pk_ref, dpk_ref, prob_ref, d2_ref,
):
    wp_ref[...] = patch_matrix(pw_ref[...])
    z = jnp.concatenate([z_ref[0].astype(F32), z_ref[1].astype(F32)], axis=1).reshape(512, 448)
    place = iota((512, 448), 0)
    tile, tile_row = place // 32, place % 32
    height = (tile_row - tile_row // 16) // 3
    used = (tile_row < 28) & (tile_row != 15)
    above = pltpu.roll(z, 10, 0)
    below = pltpu.roll(z, 502, 0)
    z = z + jnp.where((height == 1) & (tile > 0), above, 0.0)
    z = z + jnp.where((height == 7) & (tile < 15), below, 0.0)
    z = jnp.where(used & (height > 0) & (height < 8), z, 0.0).astype(BF)
    pick = iota((448, 448), 0)
    permute = one_hot(iota((448, 448), 1) == (pick % 32) * 14 + pick // 32)
    turned = dot(permute, z, NT)
    for tile_at in range(16):
        for column in range(14):
            at = ((tile_at % 2) * 14 + column) * 32
            a_ref[tile_at // 2 * 32 : tile_at // 2 * 32 + 32, at : at + 32] = turned[
                column * 32 : column * 32 + 32, tile_at * 32 : tile_at * 32 + 32
            ]
    embedded = dot(a_ref[...].astype(BF), wp_ref[...]) + pos_ref[...].astype(F32)
    gain1, gain2 = n1_ref[...].reshape(1, 384), n2_ref[...].reshape(1, 384)
    unit1, scale1, normed = norm_forward(embedded, gain1)
    pk_ref[...] = dot(normed, wqkv_ref[...]).astype(BF)
    left = iota((256, 128), 1) < 64
    zero = jnp.zeros((256, 128), BF)
    attended = []
    for pair in range(3):
        q = pk_ref[:, pair * 128 : pair * 128 + 128]
        k = pk_ref[:, 384 + pair * 128 : 384 + pair * 128 + 128]
        v = pk_ref[:, 768 + pair * 128 : 768 + pair * 128 + 128]
        both = []
        for side in range(2):
            mine = left if side == 0 else ~left
            s = dot(jnp.where(mine, q, zero), k, NT) * 0.125
            s = jnp.exp(s - jnp.max(s, axis=-1, keepdims=True))
            s = s / jnp.sum(s, axis=-1, keepdims=True)
            prob_ref[pair * 2 + side] = s
            both.append(dot(s.astype(BF), v))
        attended.append(jnp.where(left, both[0], both[1]).astype(BF))
    attended = jnp.concatenate(attended, axis=1)
    residual = embedded + dot(attended, wproj_ref[...])
    unit2, scale2, normed2 = norm_forward(residual, gain2)
    g = g_ref[...]
    out = residual
    dnormed2 = jnp.zeros((256, 384), F32)
    for part in range(2):
        cols = slice(part * 768, part * 768 + 768)
        pre = dot(normed2, w1_ref[:, cols])
        cdf = 0.5 + 0.5 * lax.erf(pre * 0.7071067811865476)
        hidden = (pre * cdf).astype(BF)
        out = out + dot(hidden, w2_ref[cols, :])
        d2 = dot(hidden, g, TN)
        for piece in range(32):
            tile_at, quarter = part * 8 + piece // 4, piece % 4
            d2_ref[quarter, tile_at * 24 : tile_at * 24 + 24, :] = d2[piece * 24 : piece * 24 + 24]
        dhidden = dot(g, w2_ref[cols, :], NT).astype(BF).astype(F32)
        slope = cdf + pre * (0.3989422804014327 * jnp.exp(-0.5 * pre * pre))
        dpre = (dhidden * slope).astype(BF)
        d1 = dot(normed2, dpre, TN).astype(BF)
        dw_ref[1 + part, :, 384 * (1 - part) : 384 * (1 - part) + 768] = d1
        dnormed2 = dnormed2 + dot(dpre, w1_ref[:, cols], NT)
    out_ref[...] = out.astype(BF)
    dw_ref[2, :, 768:] = d2_ref[0].astype(BF)
    for quarter in range(3):
        dw_ref[3, :, quarter * 384 : quarter * 384 + 384] = d2_ref[1 + quarter].astype(BF)
    dnormed2 = dnormed2.astype(BF).astype(F32)
    dres = g.astype(F32) + norm_backward(unit2, scale2, gain2, dnormed2)
    dres_bf = dres.astype(BF)
    dw_ref[1, :, :384] = dot(attended, dres_bf, TN).astype(BF)
    datt = dot(dres_bf, wproj_ref[...], NT).astype(BF)
    for pair in range(3):
        q = pk_ref[:, pair * 128 : pair * 128 + 128]
        k = pk_ref[:, 384 + pair * 128 : 384 + pair * 128 + 128]
        v = pk_ref[:, 768 + pair * 128 : 768 + pair * 128 + 128]
        da = datt[:, pair * 128 : pair * 128 + 128]
        dq, dk, dv = [], [], []
        for side in range(2):
            mine = left if side == 0 else ~left
            p = prob_ref[pair * 2 + side]
            dp = dot(jnp.where(mine, da, zero), v, NT).astype(BF).astype(F32)
            dv.append(dot(p.astype(BF), da, TN))
            ds = p * (dp - jnp.sum(dp * p, axis=-1, keepdims=True)) * 0.125
            ds = ds.astype(BF)
            dq.append(dot(ds, k))
            dk.append(dot(ds, q, TN))
        dpk_ref[:, pair * 128 : pair * 128 + 128] = jnp.where(left, dq[0], dq[1]).astype(BF)
        dpk_ref[:, 384 + pair * 128 : 384 + pair * 128 + 128] = jnp.where(left, dk[0], dk[1]).astype(BF)
        dpk_ref[:, 768 + pair * 128 : 768 + pair * 128 + 128] = jnp.where(left, dv[0], dv[1]).astype(BF)
    dpk = dpk_ref[...]
    dw_ref[0] = dot(normed, dpk, TN).astype(BF)
    dnormed = dot(dpk, wqkv_ref[...], NT).astype(BF).astype(F32)
    demb = dres + norm_backward(unit1, scale1, gain1, dnormed)
    a_ref[...] = dot(demb.astype(BF), wp_ref[...], NT)
    for tile_at in range(16):
        for column in range(14):
            at = ((tile_at % 2) * 14 + column) * 32
            r_ref[column * 32 : column * 32 + 32, tile_at * 32 : tile_at * 32 + 32] = a_ref[
                tile_at // 2 * 32 : tile_at // 2 * 32 + 32, at : at + 32
            ]
    dz = dot(r_ref[...].astype(BF), permute, TN)
    odd = tile % 2 == 1
    nothing = jnp.zeros((64, 448), F32)
    above = jnp.concatenate([nothing, dz[:448]], axis=0)
    below = jnp.concatenate([dz[64:], nothing], axis=0)
    dz = jnp.where((height == 0) & ~odd, above, dz)
    dz = jnp.where((height == 8) & odd, below, dz)
    dz = dz.reshape(16, 32, 448)
    dz_ref[0] = dz[:, :16].astype(BF)
    dz_ref[1] = dz[:, 16:].astype(BF)


def frame_step(z, g, pos, pw, n1, wqkv, wproj, n2, w1, w2):
    return pl.pallas_call(
        frame_kernel,
        out_shape=(
            jax.ShapeDtypeStruct((256, 384), BF),
            jax.ShapeDtypeStruct((2, 16, 16, 448), BF),
            jax.ShapeDtypeStruct((4, 384, 1152), BF),
        ),
        scratch_shapes=[
            pltpu.VMEM((896, 384), BF),
            pltpu.VMEM((256, 896), F32),
            pltpu.VMEM((448, 512), F32),
            pltpu.VMEM((256, 1152), BF),
            pltpu.VMEM((256, 1152), BF),
            pltpu.VMEM((6, 256, 256), F32),
            pltpu.VMEM((4, 384, 384), F32),
        ],
        name="frame_step",
    )(z, g, pos, pw, n1, wqkv, wproj, n2, w1, w2)


def flip(i):
    return i + 1 - 2 * (i % 2)


def across(i):
    return (i + 2) % 4


def mirror(i):
    return 3 - i


class Mailer:
    def __init__(self, send, recv):
        self.send, self.recv, self.count, self.copies = send, recv, 0, []

    def __call__(self, source, target, **where):
        copy = pltpu.make_async_remote_copy(
            src_ref=source,
            dst_ref=target,
            send_sem=self.send.at[self.count],
            recv_sem=self.recv.at[self.count],
            device_id=where,
            device_id_type=pl.DeviceIdType.MESH,
        )
        self.count += 1
        copy.start()
        self.copies.append(copy)
        return copy


def meet(peers):
    barrier = pltpu.get_barrier_semaphore()
    for where in peers:
        pl.semaphore_signal(barrier, inc=1, device_id=where, device_id_type=pl.DeviceIdType.MESH)
    pl.semaphore_wait(barrier, len(peers))


def accumulate(target, first, sources):
    count = sources[0].shape[0]

    def body(i, carry):
        total = target[first + i].astype(F32)
        for source in sources:
            total = total + source[i].astype(F32)
        target[first + i] = total.astype(BF)
        return carry

    lax.fori_loop(0, count, body, 0)


def reduce_kernel(
    rows_ref, w_ref, x_ref, cw_ref, sums_ref, conv_ref, pg_ref, back_ref,
    own, got, z1, z2, y1, y2, x_in, mine,
    x, rows_in, rows_f32, g_ref, part, by_space, by_dp,
    send, recv, local,
):
    space, dp = lax.axis_index("space"), lax.axis_index("dp")
    y, x_hi, core = space // 4, space // 2 % 2, space % 2
    x_lo, z = dp // 4, dp % 4
    peers = [(space + k) % 16 for k in range(1, 16)]
    dp_peers = [(dp + k) % 8 for k in range(1, 8)]

    def at(y_to=y, x_hi_to=x_hi, x_lo_to=x_lo, z_to=z, core_to=core):
        return {"dp": x_lo_to * 4 + z_to, "space": y_to * 4 + x_hi_to * 2 + core_to}

    quarters = [across(z), flip(z), mirror(z), z]
    loads = [pltpu.make_async_copy(w_ref.at[q, :, core], own.at[i], local.at[i]) for i, q in enumerate(quarters)]
    own_rows = pltpu.make_async_copy(rows_ref.at[:, space], rows_in.at[:, space], local.at[4])
    features = [pltpu.make_async_copy(x_ref.at[:, h], x.at[h], local.at[5 + h]) for h in range(7)]
    for load in loads + [own_rows] + features:
        load.start()
    meet(
        [{"dp": dp, "space": peer} for peer in peers]
        + [{"dp": peer, "space": space} for peer in dp_peers]
        + [at(x_hi_to=1 - x_hi, x_lo_to=1 - x_lo)]
    )
    mail = Mailer(send, recv)
    rows = [mail(rows_ref.at[:, peer], rows_in.at[:, space], dp=dp, space=peer) for peer in peers]
    pair = [mail(w_ref.at[q, :, 1 - core], got.at[i], **at(core_to=1 - core)) for i, q in enumerate(quarters)]
    first = []
    for i in range(4):
        loads[i].wait()
        pair[i].wait_recv()
        accumulate(own.at[i], 0, [got.at[i]])
        if i < 2:
            first.append(mail(own.at[i, 0:4], z1.at[i], **at(z_to=flip(z))))
        if i % 2 == 0:
            first.append(mail(own.at[i, 4:8], z1.at[2 + i // 2], **at(z_to=mirror(z))))
    own_rows.wait()
    for copy in rows:
        copy.wait_recv()
    rows_f32[3] = jnp.zeros((512, 128), F32)
    for batch in range(2):
        half = slice(batch * 256, batch * 256 + 256)
        for t in range(3):
            rows_f32[t, half] = rows_in[batch, :, :, t * 128 : t * 128 + 128].astype(F32).reshape(256, 128)
        rows_f32[3, half, :64] = rows_in[batch, :, :, 384:448].astype(F32).reshape(256, 64)
    for row in range(9):
        for o in range(3):
            batch, place = batch_place(row, o)
            v = jnp.concatenate(
                [rows_f32[t, pl.ds(batch * 256 + place, 16, stride=16), :] for t in range(4)], axis=1
            )
            for e in range(3):
                moved = v if e == 1 else pltpu.roll(v, 511 if e == 0 else 1, 1)
                to = (row * 9 + e * 3 + o) * 16
                pg_ref[to : to + 16, :] = moved.astype(BF)
    g_ref[...] = jnp.zeros_like(g_ref)

    def conv_rows(start, stop):
        for h in range(start, stop):
            features[h].wait()

        def body(h, carry):
            taps = pg_ref[pl.ds(pl.multiple_of(h * 144, 16), 432), :448]
            g_ref[...] += dot(taps, x[h].reshape(1536, 448), NT)
            return carry

        lax.fori_loop(start, stop, body, 0)

    conv_rows(0, 3)
    low0, high0, low1, high1 = first
    low0.wait_recv()
    accumulate(own.at[2], 0, [z1.at[0]])
    low2 = mail(own.at[2, 0:4], z2.at[0], **at(z_to=mirror(z)))
    high0.wait_recv()
    accumulate(own.at[1], 4, [z1.at[2]])
    high2 = mail(own.at[1, 4:8], z2.at[1], **at(z_to=flip(z)))
    conv_rows(3, 7)
    part[...] = jnp.zeros_like(part)
    spread = one_hot(iota((1536, 96), 0) // 16 == iota((1536, 96), 1))
    lag = iota((16, 1536), 1) % 16 - iota((16, 1536), 0) + 2
    for a in range(3):
        keep = lag == a
        sums = [
            jnp.sum(jnp.where(keep, g_ref[g * 16 : (g + 1) * 16, :], 0.0), axis=0, keepdims=True)
            for g in range(27)
        ]
        sums = [sums[(2 - b) * 9 + eo] for b in range(3) for eo in range(9)]
        total = jnp.concatenate(sums, axis=0)
        high = total.astype(BF)
        rest = (total - high.astype(F32)).astype(BF)
        part[a * 27 : (a + 1) * 27, :96] = dot(high, spread) + dot(rest, spread)
    lines = lambda i: pl.ds(pl.multiple_of(i * 8, 8), 8)
    conv_one = [mail(part.at[lines(to)], by_space.at[space], dp=dp, space=to) for to in peers]
    by_space[space] = part[lines(space), :]
    low1.wait_recv()
    low2.wait_recv()
    accumulate(own.at[3], 0, [z1.at[1], z2.at[0]])
    high1.wait_recv()
    high2.wait_recv()
    accumulate(own.at[3], 4, [z1.at[3], z2.at[1]])
    block = lambda y_of, x_of: own.at[3, pl.ds(y_of * 2 + x_of, 1)]
    low0 = mail(block(across(y), 0), y1.at[0], **at(y_to=flip(y)))
    high0 = mail(block(across(y), 1), y1.at[2], **at(y_to=mirror(y)))
    low1 = mail(block(flip(y), 0), y1.at[1], **at(y_to=flip(y)))
    high1 = mail(block(mirror(y), 1), y1.at[3], **at(y_to=mirror(y)))
    for copy in conv_one:
        copy.wait_recv()
    total = by_space[0]
    for i in range(1, 16):
        total = total + by_space[i]
    by_dp[dp] = total
    conv_two = [mail(by_dp.at[dp], by_dp.at[dp], dp=to, space=space) for to in dp_peers]
    low0.wait_recv()
    accumulate(own.at[3], mirror(y) * 2, [y1.at[0]])
    low2 = mail(block(mirror(y), 0), y2.at[0], **at(y_to=mirror(y)))
    high0.wait_recv()
    accumulate(own.at[3], flip(y) * 2 + 1, [y1.at[2]])
    high2 = mail(block(flip(y), 1), y2.at[1], **at(y_to=flip(y)))
    back_ref[...] = band_transposed(cw_ref[...].astype(F32))
    for copy in conv_two:
        copy.wait_recv()
    total = by_dp[0]
    for i in range(1, 8):
        total = total + by_dp[i]
    conv_ref[lines(space), :] = total
    conv_three = [mail(conv_ref.at[lines(space)], conv_ref.at[lines(space)], dp=dp, space=to) for to in peers]
    low1.wait_recv()
    low2.wait_recv()
    accumulate(own.at[3], y * 2, [y1.at[1], y2.at[0]])
    high1.wait_recv()
    high2.wait_recv()
    accumulate(own.at[3], y * 2 + 1, [y1.at[3], y2.at[1]])
    x_mine = x_hi * 2 + x_lo
    along_x = [
        mail(own.at[3, y * 2 + hi], x_in.at[x_mine], **at(x_hi_to=hi, x_lo_to=lo))
        for hi, lo in ((1 - x_hi, x_lo), (x_hi, 1 - x_lo), (1 - x_hi, 1 - x_lo))
    ]
    x_in[x_mine] = own[3, y * 2 + x_hi]
    for copy in along_x:
        copy.wait_recv()
    total = x_in[0].astype(F32)
    for i in range(1, 4):
        total = total + x_in[i].astype(F32)
    mine[...] = total.astype(BF)
    sums_ref[z] = total.astype(BF)
    final = [mail(mine, sums_ref.at[z], **at(z_to=to)) for to in (flip(z), mirror(z), across(z))]
    for copy in conv_three + final:
        copy.wait_recv()
    for copy in mail.copies:
        copy.wait_send()


def reduce_all(rows, weights, features, conv_weight):
    piece = (24, 1152)
    copies = 37 + 37
    vmem = pl.BlockSpec(memory_space=pltpu.VMEM)
    hbm = pl.BlockSpec(memory_space=pl.ANY)
    return pl.pallas_call(
        reduce_kernel,
        out_shape=(
            jax.ShapeDtypeStruct((4, *piece), BF),
            jax.ShapeDtypeStruct((128, 128), F32),
            jax.ShapeDtypeStruct((1296, 512), BF),
            jax.ShapeDtypeStruct((1536, 432), BF),
        ),
        in_specs=[hbm, hbm, hbm, vmem],
        out_specs=(vmem, vmem, vmem, vmem),
        scratch_shapes=[
            pltpu.VMEM((4, 8, *piece), BF),
            pltpu.VMEM((4, 8, *piece), BF),
            pltpu.VMEM((4, 4, *piece), BF),
            pltpu.VMEM((2, 4, *piece), BF),
            pltpu.VMEM((4, 1, *piece), BF),
            pltpu.VMEM((2, 1, *piece), BF),
            pltpu.VMEM((4, *piece), BF),
            pltpu.VMEM(piece, BF),
            pltpu.VMEM((7, 96, 16, 448), BF),
            pltpu.VMEM((2, 16, 16, 448), BF),
            pltpu.VMEM((4, 512, 128), F32),
            pltpu.VMEM((432, 1536), F32),
            pltpu.VMEM((128, 128), F32),
            pltpu.VMEM((16, 8, 128), F32),
            pltpu.VMEM((8, 8, 128), F32),
            pltpu.SemaphoreType.DMA((copies,)),
            pltpu.SemaphoreType.DMA((copies,)),
            pltpu.SemaphoreType.DMA((12,)),
        ],
        compiler_params=pltpu.CompilerParams(collective_id=1, has_side_effects=True),
        name="reduce_all",
    )(rows, weights.reshape(4, 8, 2, 24, 1152), features, conv_weight)


def shards(
    features, conv_weight, out_grad, pos_embed, patch_weight, norm1, qkv_weight, proj_weight,
    norm2, fc1_weight, fc2_weight,
):
    tile = features[0].transpose(0, 2, 1, 3)
    block_out, grad_rows, weights = frame_step(
        conv_forward(tile, conv_weight), out_grad[0, 0], pos_embed, patch_weight, norm1,
        qkv_weight, proj_weight, norm2, fc1_weight, fc2_weight,
    )
    sums, conv_sum, pixel_taps, back = reduce_all(grad_rows, weights, tile, conv_weight)
    feature_grad, *shares = feature_gradient(back, pixel_taps, sums)
    return (
        block_out[None, None],
        feature_grad.transpose(0, 2, 1, 3)[None],
        conv_sum[:81, :96].reshape(conv_weight.shape),
        *shares,
    )


def solution(mesh):
    placed = (
        P("dp", None, None, "space", None),
        P(),
        P("dp", "space", None, None),
        *([P()] * 8),
    )
    return jax.shard_map(
        shards,
        mesh=mesh,
        in_specs=placed,
        out_specs=(
            P("dp", "space", None, None),
            P("dp", None, None, "space", None),
            P(),
            *([P("space", None)] * 4),
        ),
        check_vma=False,
    )
```

time: 135 us -> 95.9 us (0.71); the launches traced: 133 us -> 95.5 us
  Pallas kernels: 127 us -> 93.3 us
  local copies, waits for them, and re-layouts: 5.3 us -> 1.43 us
    pallas_call x4 -> x2, Pallas kernels: 97.4 us -> 55.3 us  [the longest x1 44.9 us: reduce_all(): pl.pallas_call(reduce_kernel, out_shape=(jax.ShapeDtypeStruct((4, *piece)...]
    pallas_call x1, Pallas kernels: 13.2 us -> 21.2 us  [conv_forward(): pl.pallas_call(conv_forward_kernel, grid=(7,), out_shape=jax.ShapeDtypeSt...]
    broadcast_in_dim x2 -> x0, local copies, waits for them, and re-layouts: 2.49 us -> none  [the longest x1 1.25 us: shards(): norm1[None]]
    reshape x1 -> x0, local copies, waits for them, and re-layouts: 1.38 us -> none  [shards(): w81 = conv_weight.reshape(81, 96)]
where the time goes in v3:
time: 95.9 us; the launch traced here: 95.5 us
  Pallas kernels  93.3 us (97%)
  local copies, waits for them, and re-layouts  1.43 us (1%)
    pallas_call x1, Pallas kernels, reduce_all(): pl.pallas_call(reduce_kernel, out_shape=(jax.ShapeDtypeStruct((4, *piece)...  44.9 us
    pallas_call x1, Pallas kernels, conv_forward(): pl.pallas_call(conv_forward_kernel, grid=(7,), out_shape=jax.ShapeDtypeSt...  21.2 us
    pallas_call x1, Pallas kernels, frame_step(): pl.pallas_call(frame_kernel, out_shape=(jax.ShapeDtypeStruct((256, 384),...  16.9 us
    pallas_call x1, Pallas kernels, feature_gradient(): pl.pallas_call(feature_gradient_kernel, grid=(7,), out_shape=(jax.ShapeDt...  10.4 us

profile of v3, /device:TPU:0, one launch (start us, length us, event | category | flops | bytes accessed | tf_op | source)
XLA Modules:
  0.0 95.5 jit_solution(17215641684221162886)
XLA Ops:
  0.6 21.2 %conv_forward.1.z_ref = bf16[2,16,16,448]{3,2,1,0:T(8,128)(2,1)} custom-call(bf16[3,3,3,3,96]{4,3,2,1,0:T(4,128)(2,1)} %cw_ref.1, bf16[96,7,16,448]{3,2,1,0:T(8,128)(2,1)} %bitcast.9), custom_call_target="tpu_custom_call" | custom-call | tf_op jit(solution)/shard_map/conv_forward/pallas_call | solution.py:128
  21.8 16.9 %frame_step.1 = (bf16[256,384]{1,0:T(8,128)(2,1)}, bf16[2,16,16,448]{3,2,1,0:T(8,128)(2,1)}, bf16[4,384,1152]{2,1,0:T(8,128)(2,1)}) custom-call(bf16[2,16,16,448]{3,2,1,0:T(8,128)(2,1)} %conv_forward.1.z_ref, bf16[256,384]{1,0:T(8,128)(2,1)} %bitcast.12, bf16[256,384]{1,0:T(8,128)(2,1)} %pos_ref.1, bf16[588,384]{1,0:T(8,128)(2,1)} %pw_ref.1, f32[384]{0:T(512)} %n1_ref.1, ...), custom_call_target="tpu_custom_call" | custom-call | tf_op jit(solution)/shard_map/frame_step/pallas_call | solution.py:339
  38.7 44.9 %reduce_all.1 = (bf16[4,24,1152]{2,1,0:T(8,128)(2,1)}, f32[128,128]{1,0:T(8,128)}, bf16[1296,512]{1,0:T(8,128)(2,1)}, bf16[1536,432]{1,0:T(8,128)(2,1)}) custom-call(bf16[2,16,16,448]{3,2,1,0:T(8,128)(2,1)} %get-tuple-element.20.rows_ref, bf16[4,8,2,24,1152]{4,3,2,1,0:T(8,128)(2,1)} %bitcast.11, bf16[96,7,16,448]{3,2,1,0:T(8,128)(2,1)} %bitcast.10, ...), custom_call_target="tpu_custom_call" | custom-call | tf_op jit(solution)/shard_map/reduce_all/pallas_call | solution.py:569
  83.5 0.8 slice.3
  84.3 0.6 reshape.21
  85.0 10.4 %feature_gradient.1 = (bf16[96,7,16,448]{3,2,1,0:T(8,128)(2,1)}, f32[24,1152]{1,0:T(8,128)}, f32[24,384]{1,0:T(8,128)}, f32[24,1536]{1,0:T(8,128)}, f32[96,384]{1,0:T(8,128)}) custom-call(bf16[1536,432]{1,0:T(8,128)(2,1)} %get-tuple-element.22.band_ref, bf16[1296,512]{1,0:T(8,128)(2,1)} %get-tuple-element.23.pg_ref, ...), custom_call_target="tpu_custom_call" | custom-call | tf_op jit(solution)/shard_map/feature_gradient/pallas_call | solution.py:171
